TPU v7x, 512 devices: a whole 4x4x16 slice. The times are simulated.
512 devices in a mesh: sec: 4 (over z_hi), dev: 128 (over z_lo, y, x, core).
Axes of the slice: x: 4, y: 4, z: 16 (z_hi: 4, z_lo: 4; z = z_hi * 4 + z_lo), core: 2. Of those that a mesh axis runs over, the one named last changes fastest.
Arguments:
- queries: bfloat16 [256, 8192], P('dev', 'sec'), may hold values from -24 to 24
- cache_keys: bfloat16 [256, 4, 512, 128], P('dev', 'sec'), may hold values from -24 to 24
- cache_values: bfloat16 [256, 4, 512, 128], P('dev', 'sec'), may hold values from -48 to 48
- lengths: int32 [256], P('dev'), may hold values from 2 to 512, as said below
- out_proj: bfloat16 [4096, 8192], P('dev', 'sec'), may hold values from -0.0625 to 0.0625
- residual: bfloat16 [256, 4096], P(None, 'dev'), may hold values from -3 to 3
- norm_gain: bfloat16 [4096], replicated, may hold values from 0.5 to 1.5
- expert_ids: int32 [256, 8], replicated, may hold values from 0 to 127, all different within a row; in each aligned block of 256 rows (0 to 255, 256 to 511, ...) at most 48 rows name the same one
- gate_weights: float32 [256, 8], replicated, may hold values from 0.5 to 1.5
- owners: int32 [128], replicated, may hold values from 0 to 127, each once
- gate_proj: bfloat16 [128, 768, 4096], P('dev', 'sec'), may hold values from -0.09375 to 0.09375
- up_proj: bfloat16 [128, 768, 4096], P('dev', 'sec'), may hold values from -0.09375 to 0.09375
- down_proj: bfloat16 [128, 768, 4096], P('dev', 'sec'), may hold values from -0.21875 to 0.21875
Outputs:
- output: bfloat16 [256, 4096], P(None, 'dev')
Inputs may be any that keep to these rules, and one draw needn't show every extreme that they name: Row r's cache holds lengths[r] live positions from position 0; some row holds exactly 512. `expert_ids`: each row names 8 different experts; over all 256 rows no expert is named more than 48 times, a bound that some block reaches. Each index appears once; expert e's projections stand at index owners[e] of the expert projections.
All inputs are finite; a program needn't handle non-finite values.
Results may differ from a plain program's by a relative error of at most 0.009.
Values may be sent and summed in bfloat16 or wider, within the bound.
No kernel may reach another device: no remote copies, remote signals or barrier semaphores. Data moves between devices by JAX's collectives and lax.ppermute only.
A program may use at most 64 MiB of HBM per device.

v0:
```python
import math

import jax
import jax.numpy as jnp
from jax import lax
from jax.sharding import PartitionSpec as P

epsilon = 1e-05


def slot_targets(expert_ids, owners, capacity):
    experts = owners.shape[0]
    flat_ids = expert_ids.reshape(-1)
    one_hot = (flat_ids[:, None] == jnp.arange(experts, dtype=jnp.int32)[None, :]).astype(jnp.int32)
    before = jnp.cumsum(one_hot, axis=0) - one_hot
    position = jnp.sum(before * one_hot, axis=1)
    holder = jnp.sum(one_hot * owners[None, :], axis=1)
    return (holder * capacity + position).reshape(expert_ids.shape)


def routing_tables(expert_ids, gate_weights, owners, capacity):
    target = slot_targets(expert_ids, owners, capacity)
    places = jnp.arange(owners.shape[0] * capacity, dtype=jnp.int32)
    matched = target[None, :, :] == places[:, None, None]
    sending = jnp.any(matched, axis=2)
    weighting = jnp.sum(
        jnp.where(matched, gate_weights[None, :, :], jnp.zeros_like(gate_weights)[None, :, :]),
        axis=2,
    )
    return (sending, weighting)


def times_transpose(left, right):
    return lax.dot_general(
        left, right, (((1,), (1,)), ((), ())), preferred_element_type=jnp.float32
    )


def attend(queries, cache_keys, cache_values, lengths):
    rows, kv_heads, key_span, head_dim = cache_keys.shape
    group_size = queries.shape[1] // (kv_heads * head_dim)
    grouped = queries.reshape(rows, kv_heads, group_size, head_dim)
    scores = jnp.einsum(
        "rkgd,rktd->rkgt", grouped, cache_keys, preferred_element_type=jnp.float32
    ) / math.sqrt(head_dim)
    live_mask = (
        jnp.arange(key_span, dtype=jnp.int32)[None, None, None, :] < lengths[:, None, None, None]
    )
    scores = jnp.where(live_mask, scores, -jnp.inf)
    row_top = jnp.max(scores, axis=-1, keepdims=True)
    raised = jnp.exp(scores - row_top)
    soft_weight = (raised / jnp.sum(raised, axis=-1, keepdims=True)).astype(jnp.bfloat16)
    head_out = jnp.einsum(
        "rkgt,rktd->rkgd", soft_weight, cache_values, preferred_element_type=jnp.float32
    )
    return head_out.astype(jnp.bfloat16).reshape(rows, -1)


def root_norm(arrived, norm_gain):
    square_mean = jnp.mean(arrived * arrived, axis=-1, keepdims=True)
    return (arrived * lax.rsqrt(square_mean + epsilon) * norm_gain.astype(jnp.float32)).astype(
        jnp.bfloat16
    )


def expert_ffn(normed, gate_w, up_w, down_w):
    gate_act = times_transpose(normed, gate_w)
    up_act = times_transpose(normed, up_w)
    hidden = (jax.nn.silu(gate_act) * up_act).astype(jnp.bfloat16)
    return jnp.dot(hidden, down_w, preferred_element_type=jnp.float32)


def shards(
    queries,
    cache_keys,
    cache_values,
    lengths,
    out_proj,
    residual,
    norm_gain,
    expert_ids,
    gate_weights,
    owners,
    gate_proj,
    up_proj,
    down_proj,
):
    head_out = attend(queries, cache_keys, cache_values, lengths)
    attention_part = times_transpose(lax.all_gather(head_out, "dev", axis=0, tiled=True), out_proj)
    rows_all, top_count = expert_ids.shape
    experts = owners.shape[0]
    capacity = min(rows_all, 3 * top_count * rows_all // experts)
    col_count = out_proj.shape[0]
    sending, weighting = routing_tables(expert_ids, gate_weights, owners, capacity)
    residual_wide = residual.astype(jnp.float32)
    attention_out = lax.psum(attention_part, "sec")
    hidden_in = (residual_wide + attention_out).astype(jnp.bfloat16)
    outbound = jnp.dot(sending.astype(jnp.bfloat16), hidden_in, preferred_element_type=jnp.float32)
    outbound = outbound.astype(jnp.bfloat16).reshape(experts, capacity, col_count)
    inbound = lax.all_to_all(outbound, "dev", split_axis=0, concat_axis=2, tiled=True)
    arrived = inbound[0].astype(jnp.float32)
    normed = root_norm(arrived, norm_gain)
    expert_out = expert_ffn(normed, gate_proj[0], up_proj[0], down_proj[0])
    place_weight = jnp.sum(weighting, axis=1)
    own_weight = lax.dynamic_slice_in_dim(
        place_weight, lax.axis_index("dev") * capacity, capacity, 0
    )
    weighted = (expert_out * own_weight[:, None]).astype(jnp.bfloat16)
    returned = lax.all_to_all(
        weighted.reshape(1, capacity, weighted.shape[1]),
        "dev",
        split_axis=2,
        concat_axis=0,
        tiled=True,
    )
    moe = jnp.dot(
        sending.T.astype(jnp.bfloat16),
        returned.reshape(-1, col_count),
        preferred_element_type=jnp.float32,
    )
    summed = lax.psum(moe, "sec")
    return (residual_wide + attention_out + summed).astype(jnp.bfloat16)


def solution(mesh):
    in_specs = (
        P("dev", "sec"),
        P("dev", "sec", None, None),
        P("dev", "sec", None, None),
        P("dev"),
        P("dev", "sec"),
        P(None, "dev"),
        P(),
        P(),
        P(),
        P(),
        P("dev", "sec", None),
        P("dev", "sec", None),
        P("dev", "sec", None),
    )
    out_specs = P(None, "dev")
    return jax.shard_map(shards, mesh=mesh, in_specs=in_specs, out_specs=out_specs, check_vma=False)
```

profile of v0, /device:TPU:1, one launch (start us, length us, event | category | flops | bytes accessed | tf_op | source)
XLA Modules:
  0.0 467.0 jit_solution(8240193825732816085)
XLA Ops:
  6.5 0.0 copy-start
  6.5 0.0 all-gather.3.cloned.1.call-start
  6.5 0.8 iota_compare_fusion.4
  7.4 1.1 fusion.14
  8.5 0.2 fusion.43
  8.7 1.2 convolution_convert_fusion.1
  9.9 0.6 reshape.152
  10.5 0.0 all-gather.3.cloned.1.call-update
  10.5 0.8 copy.33
  11.4 0.1 eq.42
  11.5 0.1 eq.38
  11.6 0.1 copy.35
  11.7 0.3 fusion.23
  12.1 0.1 broadcast_add_fusion
  12.2 0.0 copy-start.9
  12.2 0.3 copy.36
  12.5 0.3 copy-done.9
  12.8 1.1 select_reduce_fusion.1
  13.9 0.1 add.41
  14.0 0.1 copy.37
  14.1 57.2 %fusion.1 = pred[6144,256]{1,0:T(8,128)(4,1)} fusion(s32[256,8]{0,1:T(8,128)S(1)} %copy.37), kind=kLoop, calls=%fused_computation.3 | loop fusion | flops 23592960 | bytes 1581056 | tf_op jit(solution)/shard_map/reduce_or | solution.py:25
  71.3 147.5 %all-gather.3.cloned.1.call-done = bf16[128,2,2048]{2,1,0:T(2,128)(2,1)} async-done(((bf16[1,2,2048]{2,1,0:T(2,128)(2,1)}), bf16[128,2,2048]{2,1,0:T(2,128)(2,1)}) %all-gather.3.cloned.1.call-update) | async-done | bytes 1048592 | tf_op jit(solution)/shard_map/all_gather | solution.py:89
  218.8 1.5 reshape.153
  220.3 0.0 copy-done.4
  220.3 0.4 fusion.44
  220.7 22.3 %psum.14 = f32[256,32]{0,1:T(8,128)S(1)} all-reduce(f32[256,32]{0,1:T(8,128)S(1)} %fusion.44), channel_id=1, replica_groups=mesh['sec'=4,'dev'=128] {'sec'}, use_global_device_ids=true, to_apply=%region_2.3 | all-reduce | flops 8192 | bytes 65536 | tf_op jit(solution)/shard_map/psum | solution.py:96
  243.0 0.0 copy-start.5
  243.0 0.6 copy-done.5
  243.6 0.0 copy-done.7
  243.6 2.4 convolution_convert_fusion
  246.1 1.1 reshape.147
  247.2 1.7 copy.50
  248.8 3.4 reshape.155
  252.3 12.5 %all-to-all-start = ((bf16[128,2,768]{2,1,0:T(2,128)(2,1)}), bf16[128,2,768]{2,1,0:T(2,128)(2,1)S(1)}, u32[]{:S(2)}, u32[]{:S(2)}) async-start(bf16[128,2,768]{2,1,0:T(2,128)(2,1)} %reshape.155), calls=%async_computation | async-start | bytes 786432 | tf_op jit(solution)/shard_map/all_to_all | solution.py:100
  264.8 0.0 copy-done.8
  264.8 0.1 reshape.151
  264.9 0.0 copy-done.10
  264.9 91.4 %select_reduce_fusion = f32[6144]{0:T(1024)S(1)} fusion(f32[256,8]{0,1:T(8,128)S(1)} %copy-done.10, s32[256,8]{0,1:T(8,128)S(1)} %copy.37), kind=kLoop, calls=%fused_computation.1 | loop fusion | flops 37742592 | bytes 40960 | tf_op jit(solution)/shard_map/reduce_sum | solution.py:104
  356.3 0.6 dynamic_slice.3
  356.9 0.0 all-to-all-done
  356.9 1.0 reshape.156
  357.9 0.0 copy-start.2
  357.9 0.6 fusion.4
  358.5 0.7 fusion.6
  359.2 0.0 copy-start.1
  359.2 0.0 copy-start.3
  359.2 1.0 copy-done.1
  360.2 0.0 copy-done.2
  360.2 1.2 fusion.10
  361.4 0.0 copy-done.3
  361.4 2.5 fusion.3
  363.9 3.9 copy.40
  367.7 0.5 broadcast.89
  368.2 23.7 %reduce.7 = bf16[4096,48]{1,0:T(8,128)(2,1)S(1)} reduce(bf16[4096,1,48]{2,1,0:T(2,128)(2,1)} %bitcast.71, bf16[]{:T(256)} %broadcast.89), dimensions={1}, to_apply=%bitcast.53.reduce_sub_computation | reduce | bytes 786434
  391.9 1.4 reshape.157
  393.3 27.3 %all_to_all.24 = bf16[128,2,768]{2,1,0:T(2,128)(2,1)S(1)} all-to-all(bf16[128,2,768]{2,1,0:T(2,128)(2,1)S(1)} %reshape.157), channel_id=1, replica_groups=mesh['sec'=4,'dev'=128] {'dev'}, dimensions={0} | all-to-all | bytes 786432 | tf_op jit(solution)/shard_map/all_to_all | solution.py:109
  420.6 4.1 reshape.158
  424.7 4.6 copy.41
  429.3 1.3 all_to_all.20
  430.5 3.4 copy.42
  433.9 2.8 reshape.149
  436.7 2.3 fusion.45
  439.0 20.3 %psum.15 = f32[256,32]{0,1:T(8,128)S(1)} all-reduce(f32[256,32]{0,1:T(8,128)S(1)} %fusion.45), channel_id=1, replica_groups=mesh['sec'=4,'dev'=128] {'sec'}, use_global_device_ids=true, to_apply=%region_10.11 | all-reduce | flops 8192 | bytes 65536 | tf_op jit(solution)/shard_map/psum | solution.py:121
  459.3 0.6 add_convert_fusion
  (12 shorter events, 0.1 us)
Async XLA Ops:
  6.5 354.8 %copy-start = (bf16[1,192,4096]{2,1,0:T(8,128)(2,1)S(1)}, bf16[1,192,4096]{2,1,0:T(8,128)(2,1)}, u32[]{:S(2)}) copy-start(bf16[1,192,4096]{2,1,0:T(8,128)(2,1)} %param.25) | copy-start | bytes 4718596
  6.5 212.3 %all-gather.3.cloned.1.call-start = ((), (), s32[]{:S(2)}) async-start(), calls=%async_computation.2 | async-start | bytes 1056768 | tf_op jit(solution)/shard_map/all_gather | solution.py:89
  12.2 0.7 copy-start.9
  14.1 206.2 %copy-start.4 = (bf16[32,2048]{1,0:T(8,128)(2,1)S(1)}, bf16[32,2048]{1,0:T(8,128)(2,1)}, u32[]{:S(2)}) copy-start(bf16[32,2048]{1,0:T(8,128)(2,1)} %param.17) | copy-start | bytes 393220
  71.3 172.3 %copy-start.7 = (bf16[256,32]{0,1:T(8,128)(2,1)S(1)}, bf16[256,32]{0,1:T(8,128)(2,1)}, u32[]{:S(2)}) copy-start(bf16[256,32]{0,1:T(8,128)(2,1)} %param.18) | copy-start | bytes 49156
  243.0 0.6 copy-start.5
  248.8 16.0 %copy-start.8 = (bf16[4096]{0:T(1024)(128)(2,1)S(1)}, bf16[4096]{0:T(1024)(128)(2,1)}, u32[]{:S(2)}) copy-start(bf16[4096]{0:T(1024)(128)(2,1)} %param.19) | copy-start | bytes 24580
  248.8 16.1 %copy-start.10 = (f32[256,8]{0,1:T(8,128)S(1)}, f32[256,8]{0,1:T(8,128)}, u32[]{:S(2)}) copy-start(f32[256,8]{0,1:T(8,128)} %param.21) | copy-start | bytes 24580
  252.3 104.6 %all-to-all-start = ((bf16[128,2,768]{2,1,0:T(2,128)(2,1)}), bf16[128,2,768]{2,1,0:T(2,128)(2,1)S(1)}, u32[]{:S(2)}, u32[]{:S(2)}) async-start(bf16[128,2,768]{2,1,0:T(2,128)(2,1)} %reshape.155), calls=%async_computation | async-start | bytes 786432 | tf_op jit(solution)/shard_map/all_to_all | solution.py:100
  357.9 2.3 copy-start.2
  359.2 1.0 copy-start.1
  359.2 2.2 copy-start.3
  436.7 22.6 %copy-start.6 = (f32[256,32]{0,1:T(8,128)S(1)}, f32[256,32]{0,1:T(8,128)}, u32[]{:S(2)}) copy-start(f32[256,32]{0,1:T(8,128)} %copy-done.5) | copy-start | bytes 98308
Sparse Core Ops, SparseCore 0:
  10.7 208.1 all-gather.2
where the time goes:
time: 476 us; the launch traced here: 467 us
  other arithmetic  177 us (37%)
  waiting for transfers between devices  148 us (31%)
  blocking collectives  70 us (15%)
  local copies, waits for them, and re-layouts  35.3 us (7%)
  between operations  13.9 us (3%)
  starting transfers between devices  12.5 us (3%)
  matrix products  11.1 us (2%)
    all_gather x1, waiting for transfers between devices, shards(): lax.all_gather(head_out, 'dev', axis=0, tiled=True)  148 us
    reduce_sum x1, other arithmetic, shards(): place_weight = jnp.sum(weighting, axis=1)  91.4 us
    reduce_or x1, other arithmetic, routing_tables(): sending = jnp.any(matched, axis=2)  57.2 us
    all_to_all x1, blocking collectives, shards(): lax.all_to_all(weighted.reshape(1, capacity, weighted.shape[1]), 'dev', s...  27.3 us
    unnamed x1, other arithmetic  23.7 us
    psum x1, blocking collectives, shards(): attention_out = lax.psum(attention_part, 'sec')  22.3 us
    psum x1, blocking collectives, shards(): summed = lax.psum(moe, 'sec')  20.3 us
    unnamed x30, local copies, waits for them, and re-layouts  15.2 us
  transfers between devices with their start and end apart: 2, of which 1 were waited for; matrix products, arithmetic and copies ran while one was open for 33% of the time, Pallas kernels for 0%

commit v1 on v0

v1 whole, which is shorter than its diff:
```python
import math

import jax
import jax.numpy as jnp
from jax import lax
from jax.experimental import pallas as pl
from jax.experimental.pallas import tpu as pltpu
from jax.sharding import PartitionSpec as P

epsilon = 1e-05

BANDS = 4
PART = 12
ROW = 16


def attend(queries, cache_keys, cache_values, lengths):
    rows, kv_heads, key_span, head_dim = cache_keys.shape
    group_size = queries.shape[1] // (kv_heads * head_dim)
    grouped = queries.reshape(rows, kv_heads, group_size, head_dim)
    scores = jnp.einsum(
        "rkgd,rktd->rkgt", grouped, cache_keys, preferred_element_type=jnp.float32
    ) / math.sqrt(head_dim)
    live_mask = (
        jnp.arange(key_span, dtype=jnp.int32)[None, None, None, :] < lengths[:, None, None, None]
    )
    scores = jnp.where(live_mask, scores, -jnp.inf)
    row_top = jnp.max(scores, axis=-1, keepdims=True)
    raised = jnp.exp(scores - row_top)
    soft_weight = (raised / jnp.sum(raised, axis=-1, keepdims=True)).astype(jnp.bfloat16)
    head_out = jnp.einsum(
        "rkgt,rktd->rkgd", soft_weight, cache_values, preferred_element_type=jnp.float32
    )
    return head_out.astype(jnp.bfloat16).reshape(rows, -1)


def nt_dot(left, right):
    return lax.dot_general(
        left, right, (((1,), (1,)), ((), ())), preferred_element_type=jnp.float32
    )


def iota(shape, dim):
    return lax.broadcasted_iota(jnp.int32, shape, dim)


def one_hot(condition):
    return jnp.where(condition, 1.0, 0.0).astype(jnp.bfloat16)


def routing_kernel(me_ref, ids_ref, gates_ref, owners_ref, table_ref, weight_ref, swap_ref, slot_ref):
    top_count, rows = ids_ref.shape
    experts = owners_ref.shape[1]
    me = me_ref[0]
    ids = ids_ref[...]
    owners = owners_ref[...]
    named = jnp.zeros((experts, rows), jnp.float32)
    expert_at = iota((experts, rows), 0)
    for k in range(top_count):
        named = jnp.where(ids[k : k + 1, :] == expert_at, 1.0, named)
    holds = one_hot(owners == iota((experts, experts), 0))
    routed = jnp.dot(holds, named.astype(jnp.bfloat16), preferred_element_type=jnp.float32)
    earlier = one_hot(iota((rows, rows), 0) < iota((rows, rows), 1))
    before = jnp.dot(routed.astype(jnp.bfloat16), earlier, preferred_element_type=jnp.float32)
    slots = jnp.where(routed > 0.5, before, -1.0)
    slot_ref[...] = slots

    mine = jnp.sum(
        jnp.where(owners == me, iota(owners.shape, 1), 0), axis=1, keepdims=True
    )
    row_gate = jnp.sum(jnp.where(ids == mine, gates_ref[...], 0.0), axis=0, keepdims=True)
    row_slot = jnp.sum(jnp.where(iota(slots.shape, 0) == me, slots, 0.0), axis=0, keepdims=True)
    at = iota((BANDS * ROW, rows), 0)
    place = jnp.where(at % ROW < PART, at // ROW * PART + at % ROW, rows + 1).astype(jnp.float32)
    weight_ref[...] = jnp.sum(jnp.where(row_slot == place, row_gate, 0.0), axis=1, keepdims=True)

    lanes = swap_ref.shape[0]
    source = iota((lanes, lanes), 0)
    target = iota((lanes, lanes), 1)
    swapped = target % 32 + target // 128 * 32 + target // 32 % 4 * 128
    swap_ref[...] = one_hot(source == swapped)

    row_at = iota((ROW, rows), 0)
    row_place = jnp.where(row_at < PART, row_at, 4 * rows).astype(jnp.float32)

    def fill(expert, carry):
        slot = slot_ref[pl.ds(expert, 1), :]
        for band in range(BANDS):
            table_ref[expert, :, band * rows : (band + 1) * rows] = one_hot(
                slot - float(band * PART) == row_place
            )
        return carry

    lax.fori_loop(0, experts, fill, 0, unroll=4)


def routing(expert_ids, gate_weights, owners, me):
    rows, top_count = expert_ids.shape
    experts = owners.shape[0]
    vmem = pl.BlockSpec(memory_space=pltpu.VMEM)
    return pl.pallas_call(
        routing_kernel,
        out_shape=(
            jax.ShapeDtypeStruct((experts, ROW, BANDS * rows), jnp.bfloat16),
            jax.ShapeDtypeStruct((BANDS * ROW, 1), jnp.float32),
            jax.ShapeDtypeStruct((512, 512), jnp.bfloat16),
        ),
        in_specs=[pl.BlockSpec(memory_space=pltpu.SMEM), vmem, vmem, vmem],
        out_specs=(vmem, vmem, vmem),
        scratch_shapes=[pltpu.VMEM((experts, rows), jnp.float32)],
        name="routing",
    )(me.reshape(1), expert_ids.T, gate_weights.T, owners.reshape(1, -1))


def dispatch_kernel(parts_ref, residual_ref, table_ref, send_ref, base_ref, wide_ref):
    groups, cols, rows = parts_ref.shape
    source = iota((rows, rows), 0)
    target = iota((rows, rows), 1)
    half = rows // 2
    order = one_hot(source == target // 2 % 2 * half + target // 4 * 2 + target % 2)
    parts = jnp.dot(
        parts_ref[...].reshape(groups * cols, rows), order, preferred_element_type=jnp.float32
    )
    attention = parts[:cols]
    for group in range(1, groups):
        attention = attention + parts[group * cols : (group + 1) * cols]
    base = residual_ref[...].astype(jnp.float32) + attention
    base_ref[...] = base
    hidden_in = base.astype(jnp.bfloat16)
    wide_ref[...] = jnp.zeros(wide_ref.shape, jnp.bfloat16)
    for band in range(BANDS):
        wide_ref[band * cols : (band + 1) * cols, band * rows : (band + 1) * rows] = hidden_in
    experts = table_ref.shape[0]
    table = table_ref[...].reshape(experts * ROW, BANDS * rows)
    sent = nt_dot(table, wide_ref[...]).astype(jnp.bfloat16)
    send_ref[...] = sent.reshape(experts, ROW, BANDS * cols)[:, :PART, :]


def dispatch(parts, residual, table):
    groups, cols, rows = parts.shape
    experts = table.shape[0]
    vmem = pl.BlockSpec(memory_space=pltpu.VMEM)
    return pl.pallas_call(
        dispatch_kernel,
        out_shape=(
            jax.ShapeDtypeStruct((experts, PART, BANDS * cols), jnp.bfloat16),
            jax.ShapeDtypeStruct((cols, rows), jnp.float32),
        ),
        in_specs=[vmem] * 3,
        out_specs=(vmem, vmem),
        scratch_shapes=[pltpu.VMEM((BANDS * cols, BANDS * rows), jnp.bfloat16)],
        name="dispatch",
    )(parts, residual, table)


def expert_kernel(
    inbound_ref, gain_ref, weight_ref, swap_ref, gate_ref, up_ref, down_ref, send_ref, fold_ref, flat_ref
):
    devices = inbound_ref.shape[0]
    width = gain_ref.shape[1]
    tiles = devices // BANDS
    fold_ref[...] = jnp.zeros(fold_ref.shape, fold_ref.dtype)
    for device in range(devices):
        tile, lane = device // BANDS, device % BANDS
        fold_ref[tile * ROW : tile * ROW + PART, lane * 128 : (lane + 1) * 128] = inbound_ref[device]
    swap = swap_ref[...]
    turned = jnp.dot(fold_ref[...], swap, preferred_element_type=jnp.float32)
    for tile in range(tiles):
        for band in range(BANDS):
            flat_ref[band * ROW : (band + 1) * ROW, tile * 128 : (tile + 1) * 128] = turned[
                tile * ROW : (tile + 1) * ROW, band * 128 : (band + 1) * 128
            ]
    arrived = flat_ref[...]
    square_mean = jnp.sum(arrived * arrived, axis=1, keepdims=True) / width
    normed = (
        arrived * lax.rsqrt(square_mean + epsilon) * gain_ref[...].astype(jnp.float32)
    ).astype(jnp.bfloat16)
    gate_act = nt_dot(normed, gate_ref[...])
    up_act = nt_dot(normed, up_ref[...])
    hidden = (jax.nn.silu(gate_act) * up_act).astype(jnp.bfloat16)
    expert_out = jnp.dot(hidden, down_ref[...], preferred_element_type=jnp.float32)
    weighted = (expert_out * weight_ref[...]).astype(jnp.bfloat16)
    for tile in range(tiles):
        for band in range(BANDS):
            fold_ref[tile * ROW : (tile + 1) * ROW, band * 128 : (band + 1) * 128] = weighted[
                band * ROW : (band + 1) * ROW, tile * 128 : (tile + 1) * 128
            ]
    back = jnp.dot(fold_ref[...], swap, preferred_element_type=jnp.float32).astype(jnp.bfloat16)
    for device in range(devices):
        tile, lane = device // BANDS, device % BANDS
        send_ref[device] = back[tile * ROW : tile * ROW + PART, lane * 128 : (lane + 1) * 128]


def expert_layer(inbound, norm_gain, weight, swap, gate_proj, up_proj, down_proj):
    devices = inbound.shape[0]
    width = norm_gain.shape[0]
    vmem = pl.BlockSpec(memory_space=pltpu.VMEM)
    return pl.pallas_call(
        expert_kernel,
        out_shape=jax.ShapeDtypeStruct(inbound.shape, jnp.bfloat16),
        in_specs=[vmem] * 7,
        out_specs=vmem,
        scratch_shapes=[
            pltpu.VMEM((devices // BANDS * ROW, 512), jnp.bfloat16),
            pltpu.VMEM((BANDS * ROW, width), jnp.float32),
        ],
        name="expert_layer",
    )(inbound, norm_gain.reshape(1, -1), weight, swap, gate_proj, up_proj, down_proj)


def combine_kernel(returned_ref, table_ref, parts_ref, rows_ref):
    experts = returned_ref.shape[0]
    cols, rows = parts_ref.shape[1:]
    rows_ref[...] = jnp.zeros(rows_ref.shape, rows_ref.dtype)
    for expert in range(experts):
        rows_ref[expert * ROW : expert * ROW + PART, :] = returned_ref[expert]
    table = table_ref[...].reshape(experts * ROW, BANDS * rows)
    mixed = lax.dot_general(
        rows_ref[...], table, (((0,), (0,)), ((), ())), preferred_element_type=jnp.float32
    )
    moe = mixed[:cols, :rows]
    for band in range(1, BANDS):
        moe = moe + mixed[band * cols : (band + 1) * cols, band * rows : (band + 1) * rows]
    moe = moe.astype(jnp.bfloat16)
    for group in range(parts_ref.shape[0]):
        parts_ref[group] = moe


def combine(returned, table, groups, cols, rows):
    experts = returned.shape[0]
    vmem = pl.BlockSpec(memory_space=pltpu.VMEM)
    return pl.pallas_call(
        combine_kernel,
        out_shape=jax.ShapeDtypeStruct((groups, cols, rows), jnp.bfloat16),
        in_specs=[vmem] * 2,
        out_specs=vmem,
        scratch_shapes=[pltpu.VMEM((experts * ROW, BANDS * cols), jnp.bfloat16)],
        name="combine",
    )(returned, table)


def shards(
    queries,
    cache_keys,
    cache_values,
    lengths,
    out_proj,
    residual,
    norm_gain,
    expert_ids,
    gate_weights,
    owners,
    gate_proj,
    up_proj,
    down_proj,
):
    rows, cols = residual.shape
    groups = lax.axis_size("sec")
    devices = lax.axis_size("dev")
    chips = devices // 2
    me = lax.axis_index("dev")
    table, weight, swap = routing(expert_ids, gate_weights, owners, me)

    head_out = attend(queries, cache_keys, cache_values, lengths)
    same_core = [[2 * chip + core for chip in range(chips)] for core in range(2)]
    swap_core = [(device, device ^ 1) for device in range(devices)]
    gathered = lax.all_to_all(
        jnp.broadcast_to(head_out[None], (chips,) + head_out.shape),
        "dev",
        0,
        0,
        tiled=True,
        axis_index_groups=same_core,
    )
    gathered = gathered.reshape(-1, head_out.shape[1])
    other = lax.ppermute(gathered, "dev", swap_core)
    own_part = nt_dot(out_proj, gathered).astype(jnp.bfloat16)
    other_part = nt_dot(out_proj, other).astype(jnp.bfloat16)
    first = me % 2 == 0
    part = jnp.concatenate(
        [jnp.where(first, own_part, other_part), jnp.where(first, other_part, own_part)], axis=1
    )
    parts = lax.all_to_all(
        jnp.broadcast_to(part[None], (groups,) + part.shape), "sec", 0, 0, tiled=True
    )
    outbound, base = dispatch(parts, residual.T, table)
    inbound = lax.all_to_all(outbound, "dev", 0, 0, tiled=True)
    weighted = expert_layer(
        inbound, norm_gain, weight, swap, gate_proj[0], up_proj[0], down_proj[0]
    )
    returned = lax.all_to_all(weighted, "dev", 0, 0, tiled=True)
    moe_parts = lax.all_to_all(
        combine(returned, table, groups, cols, rows), "sec", 0, 0, tiled=True
    )
    moe = jnp.sum(moe_parts.astype(jnp.float32), axis=0)
    return (base + moe).astype(jnp.bfloat16).T


def solution(mesh):
    in_specs = (
        P("dev", "sec"),
        P("dev", "sec", None, None),
        P("dev", "sec", None, None),
        P("dev"),
        P("dev", "sec"),
        P(None, "dev"),
        P(),
        P(),
        P(),
        P(),
        P("dev", "sec", None),
        P("dev", "sec", None),
        P("dev", "sec", None),
    )
    out_specs = P(None, "dev")
    return jax.shard_map(shards, mesh=mesh, in_specs=in_specs, out_specs=out_specs, check_vma=False)
```

time: 476 us -> 147 us (0.31); the launches traced: 467 us -> 147 us
  other arithmetic: 177 us -> 1.41 us
  waiting for transfers between devices: 148 us -> 26.1 us
  local copies, waits for them, and re-layouts: 35.3 us -> 3.37 us
  Pallas kernels: 0 us -> 18.6 us
  between operations: 13.9 us -> 0.1 us
  starting transfers between devices: 12.5 us -> 23.7 us
  matrix products: 11.1 us -> 2.78 us
    all_gather x1 -> x0, waiting for transfers between devices: 148 us -> none  [shards(): lax.all_gather(head_out, 'dev', axis=0, tiled=True)]
    reduce_sum x3 -> x1, other arithmetic: 93 us -> 0.01 us  [shards(): moe = jnp.sum(moe_parts.astype(jnp.float32), axis=0)]
    reduce_or x1 -> x0, other arithmetic: 57.2 us -> none  [routing_tables(): sending = jnp.any(matched, axis=2)]
    all_to_all x1 -> x3, blocking collectives: 27.3 us -> 70.6 us  [the longest x1 29.3 us: shards(): lax.all_to_all(jnp.broadcast_to(head_out[None], (chips,) + head_out.shape...]
    psum x2 -> x0, blocking collectives: 42.6 us -> none  [the longest x1 22.3 us: shards(): attention_out = lax.psum(attention_part, 'sec')]
    all_to_all x1 -> x2, waiting for transfers between devices: 0.01 us -> 24.9 us  [the longest x1 17.6 us: shards(): inbound = lax.all_to_all(outbound, 'dev', 0, 0, tiled=True)]
    unnamed x1 -> x0, other arithmetic: 23.7 us -> none
    pallas_call x0 -> x4, Pallas kernels: none -> 18.6 us  [the longest x1 5.86 us: expert_layer(): pl.pallas_call(expert_kernel, out_shape=jax.ShapeDtypeStruct(inbound.shap...]
  transfers between devices with their start and end apart: 2 -> 3, of which waited for: 1 -> 3; matrix products, arithmetic and copies ran while one was open for 33% -> 1% of each run, Pallas kernels for 0% -> 3%
where the time goes in v1:
time: 147 us
  blocking collectives  70.6 us (48%)
  waiting for transfers between devices  26.1 us (18%)
  starting transfers between devices  23.7 us (16%)
  Pallas kernels  18.6 us (13%)
  local copies, waits for them, and re-layouts  3.37 us (2%)
  matrix products  2.78 us (2%)
    all_to_all x1, blocking collectives, shards(): lax.all_to_all(jnp.broadcast_to(head_out[None], (chips,) + head_out.shape...  29.3 us
    all_to_all x1, blocking collectives, shards(): returned = lax.all_to_all(weighted, 'dev', 0, 0, tiled=True)  25.6 us
    all_to_all x1, waiting for transfers between devices, shards(): inbound = lax.all_to_all(outbound, 'dev', 0, 0, tiled=True)  17.6 us
    all_to_all x1, blocking collectives, shards(): lax.all_to_all(combine(returned, table, groups, cols, rows), 'sec', 0, 0,...  15.6 us
    all_to_all x1, starting transfers between devices, shards(): lax.all_to_all(jnp.broadcast_to(part[None], (groups,) + part.shape), 'sec...  12.1 us
    all_to_all x1, starting transfers between devices, shards(): inbound = lax.all_to_all(outbound, 'dev', 0, 0, tiled=True)  7.63 us
    all_to_all x1, waiting for transfers between devices, shards(): lax.all_to_all(jnp.broadcast_to(part[None], (groups,) + part.shape), 'sec...  7.29 us
    pallas_call x1, Pallas kernels, expert_layer(): pl.pallas_call(expert_kernel, out_shape=jax.ShapeDtypeStruct(inbound.shap...  5.86 us
  transfers between devices with their start and end apart: 3, of which 3 were waited for; matrix products, arithmetic and copies ran while one was open for 1% of the time, Pallas kernels for 3%

profile of v1, /device:TPU:1, one launch (start us, length us, event | category | flops | bytes accessed | tf_op | source)
XLA Modules:
  0.0 146.6 jit_solution(6808728128654492383)
XLA Ops:
  0.0 0.0 copy-start
  0.0 0.8 iota_compare_fusion
  0.8 0.2 copy-done
  1.0 1.0 fusion.11
  2.0 0.0 copy-start.2
  2.0 1.2 fusion.4
  3.2 0.3 broadcast_in_dim.32
  3.5 29.3 %all_to_all.25 = bf16[64,2,2048]{2,1,0:T(2,128)(2,1)S(1)} all-to-all(bf16[64,2,2048]{2,1,0:T(2,128)(2,1)S(1)} %broadcast_in_dim.32), channel_id=1, replica_groups={{0,2,4,6,8,10,12,14,16,18,20,22,24,26,28,30,32,34,36,38,40,42,44,46,48,..., dimensions={0} | all-to-all | bytes 1048576 | tf_op jit(solution)/shard_map/all_to_all | solution.py:267
  32.8 0.2 reshape.73
  33.0 3.9 %collective-permute-start = (bf16[128,2048]{1,0:T(8,128)(2,1)S(1)}, bf16[128,2048]{1,0:T(8,128)(2,1)S(1)}, u32[]{:S(2)}, u32[]{:S(2)}) collective-permute-start(bf16[128,2048]{1,0:T(8,128)(2,1)S(1)} %reshape.73), channel_id=1, source_target_pairs={{0,1},{1,0},{2,3},{3,2},{4,5},{5,4},{6,7},{7,6},{8,9},{9,8},{10,11... | collective-permute-start | bytes 1572872 | tf_op jit(solution)/shard_map/ppermute | solution.py:276
  37.0 0.0 copy-done.2
  37.0 0.3 convolution_convert_fusion.1
  37.2 1.2 collective-permute-done
  38.5 0.3 select_bitcast_fusion.1
  38.8 0.6 broadcast_in_dim.33
  39.4 12.1 %all-to-all-start.1 = ((bf16[4,32,256]{2,1,0:T(8,128)(2,1)}), bf16[4,32,256]{2,1,0:T(8,128)(2,1)S(1)}, u32[]{:S(2)}, u32[]{:S(2)}) async-start(bf16[4,32,256]{2,1,0:T(8,128)(2,1)} %broadcast_in_dim.33), calls=%async_computation.1 | async-start | bytes 131072 | tf_op jit(solution)/shard_map/all_to_all | solution.py:283
  51.5 4.4 %routing.1 = (bf16[128,16,1024]{2,1,0:T(8,128)(2,1)}, f32[64,1]{1,0:T(8,128)}, bf16[512,512]{1,0:T(8,128)(2,1)}) custom-call(s32[1]{0:T(128)} %bitcast.5.me_ref, s32[8,256]{1,0:T(8,128)} %bitcast.42, f32[8,256]{1,0:T(8,128)} %bitcast.43, s32[1,128]{1,0:T(1,128)} %bitcast.45), custom_call_target="tpu_custom_call" | custom-call | tf_op jit(solution)/shard_map/routing/pallas_call | solution.py:101
  55.9 7.3 %all-to-all-done.1.parts_ref = bf16[4,32,256]{2,1,0:T(8,128)(2,1)S(1)} async-done(((bf16[4,32,256]{2,1,0:T(8,128)(2,1)}), bf16[4,32,256]{2,1,0:T(8,128)(2,1)S(1)}, u32[]{:S(2)}, u32[]{:S(2)}) %all-to-all-start.1) | async-done | bytes 65568 | tf_op jit(solution)/shard_map/all_to_all | solution.py:283
  63.2 0.0 copy-start.3
  63.2 0.6 copy-done.3
  63.8 0.0 copy-start.5
  63.8 4.5 %dispatch.1 = (bf16[128,12,128]{2,1,0:T(8,128)(2,1)}, f32[32,256]{1,0:T(8,128)}) custom-call(bf16[4,32,256]{2,1,0:T(8,128)(2,1)} %copy-done.3, bf16[32,256]{1,0:T(8,128)(2,1)} %bitcast.41, bf16[128,16,1024]{2,1,0:T(8,128)(2,1)} %get-tuple-element.10.table_ref), custom_call_target="tpu_custom_call" | custom-call | tf_op jit(solution)/shard_map/dispatch/pallas_call | solution.py:143
  68.4 7.6 %all-to-all-start.2 = ((bf16[128,12,128]{2,1,0:T(8,128)(2,1)}), bf16[128,12,128]{2,1,0:T(8,128)(2,1)S(1)}, u32[]{:S(2)}, u32[]{:S(2)}) async-start(bf16[128,12,128]{2,1,0:T(8,128)(2,1)} %get-tuple-element.12), calls=%async_computation.2 | async-start | bytes 1048576 | tf_op jit(solution)/shard_map/all_to_all | solution.py:287
  76.0 0.0 copy-done.5
  76.0 0.6 reshape.76.gain_ref
  76.6 17.6 %all-to-all-done.2.inbound_ref = bf16[128,12,128]{2,1,0:T(8,128)(2,1)S(1)} async-done(((bf16[128,12,128]{2,1,0:T(8,128)(2,1)}), bf16[128,12,128]{2,1,0:T(8,128)(2,1)S(1)}, u32[]{:S(2)}, u32[]{:S(2)}) %all-to-all-start.2) | async-done | bytes 393248 | tf_op jit(solution)/shard_map/all_to_all | solution.py:287
  94.2 0.0 copy-start.1
  94.2 0.8 copy-done.1
  95.0 5.9 %expert_layer.1 = bf16[128,12,128]{2,1,0:T(8,128)(2,1)} custom-call(bf16[128,12,128]{2,1,0:T(8,128)(2,1)} %copy-done.1, bf16[1,4096]{1,0:T(2,128)(2,1)} %reshape.76.gain_ref, f32[64,1]{1,0:T(8,128)} %get-tuple-element.13.weight_ref, bf16[512,512]{1,0:T(8,128)(2,1)} %get-tuple-element.14.swap_ref, bf16[192,4096]{1,0:T(8,128)(2,1)} %bitcast.37, ...), custom_call_target="tpu_custom_call" | custom-call | tf_op jit(solution)/shard_map/expert_layer/pallas_call | solution.py:198
  100.9 25.6 %all_to_all.26.returned_ref = bf16[128,12,128]{2,1,0:T(8,128)(2,1)} all-to-all(bf16[128,12,128]{2,1,0:T(8,128)(2,1)} %expert_layer.1), channel_id=1, replica_groups=mesh['sec'=4,'dev'=128] {'dev'}, dimensions={0} | all-to-all | bytes 786432 | tf_op jit(solution)/shard_map/all_to_all | solution.py:291
  126.5 0.0 copy-start.4
  126.5 3.8 %combine.1 = bf16[4,32,256]{2,1,0:T(8,128)(2,1)} custom-call(bf16[128,12,128]{2,1,0:T(8,128)(2,1)} %all_to_all.26.returned_ref, bf16[128,16,1024]{2,1,0:T(8,128)(2,1)} %get-tuple-element.10.table_ref), custom_call_target="tpu_custom_call" | custom-call | tf_op jit(solution)/shard_map/combine/pallas_call | solution.py:232
  130.4 15.6 %all_to_all.27 = bf16[4,32,256]{2,1,0:T(8,128)(2,1)S(1)} all-to-all(bf16[4,32,256]{2,1,0:T(8,128)(2,1)} %combine.1), channel_id=1, replica_groups=mesh['sec'=4,'dev'=128] {'sec'}, dimensions={0} | all-to-all | bytes 131072 | tf_op jit(solution)/shard_map/all_to_all | solution.py:292
  146.0 0.0 copy-done.4
  146.0 0.6 fusion.8
  (3 shorter events, 0.0 us)
Async XLA Ops:
  0.0 1.0 copy-start
  2.0 35.0 %copy-start.2 = (bf16[32,2048]{1,0:T(8,128)(2,1)S(1)}, bf16[32,2048]{1,0:T(8,128)(2,1)}, u32[]{:S(2)}) copy-start(bf16[32,2048]{1,0:T(8,128)(2,1)} %param.17) | copy-start | bytes 393220
  33.0 5.5 %collective-permute-start = (bf16[128,2048]{1,0:T(8,128)(2,1)S(1)}, bf16[128,2048]{1,0:T(8,128)(2,1)S(1)}, u32[]{:S(2)}, u32[]{:S(2)}) collective-permute-start(bf16[128,2048]{1,0:T(8,128)(2,1)S(1)} %reshape.73), channel_id=1, source_target_pairs={{0,1},{1,0},{2,3},{3,2},{4,5},{5,4},{6,7},{7,6},{8,9},{9,8},{10,11... | collective-permute-start | bytes 1572872 | tf_op jit(solution)/shard_map/ppermute | solution.py:276
  39.4 23.8 %all-to-all-start.1 = ((bf16[4,32,256]{2,1,0:T(8,128)(2,1)}), bf16[4,32,256]{2,1,0:T(8,128)(2,1)S(1)}, u32[]{:S(2)}, u32[]{:S(2)}) async-start(bf16[4,32,256]{2,1,0:T(8,128)(2,1)} %broadcast_in_dim.33), calls=%async_computation.1 | async-start | bytes 131072 | tf_op jit(solution)/shard_map/all_to_all | solution.py:283
  63.2 0.6 copy-start.3
  63.8 12.2 %copy-start.5 = (bf16[4096]{0:T(1024)(128)(2,1)S(1)}, bf16[4096]{0:T(1024)(128)(2,1)}, u32[]{:S(2)}) copy-start(bf16[4096]{0:T(1024)(128)(2,1)} %param.19) | copy-start | bytes 24580
  68.4 25.8 %all-to-all-start.2 = ((bf16[128,12,128]{2,1,0:T(8,128)(2,1)}), bf16[128,12,128]{2,1,0:T(8,128)(2,1)S(1)}, u32[]{:S(2)}, u32[]{:S(2)}) async-start(bf16[128,12,128]{2,1,0:T(8,128)(2,1)} %get-tuple-element.12), calls=%async_computation.2 | async-start | bytes 1048576 | tf_op jit(solution)/shard_map/all_to_all | solution.py:287
  94.2 0.8 copy-start.1
  126.5 19.5 %copy-start.4 = (f32[32,256]{1,0:T(8,128)S(1)}, f32[32,256]{1,0:T(8,128)}, u32[]{:S(2)}) copy-start(f32[32,256]{1,0:T(8,128)} %get-tuple-element.11) | copy-start | bytes 98308

commit v2 on v1

v2 whole, which is shorter than its diff:
```python
import math

import jax
import jax.numpy as jnp
from jax import lax
from jax.experimental import pallas as pl
from jax.experimental.pallas import tpu as pltpu
from jax.sharding import PartitionSpec as P

epsilon = 1e-05

PLANES = 4
PLANE = 32
CAP = 48


def attend(queries, cache_keys, cache_values, lengths):
    rows, kv_heads, key_span, head_dim = cache_keys.shape
    group_size = queries.shape[1] // (kv_heads * head_dim)
    grouped = queries.reshape(rows, kv_heads, group_size, head_dim)
    scores = jnp.einsum(
        "rkgd,rktd->rkgt", grouped, cache_keys, preferred_element_type=jnp.float32
    ) / math.sqrt(head_dim)
    live_mask = (
        jnp.arange(key_span, dtype=jnp.int32)[None, None, None, :] < lengths[:, None, None, None]
    )
    scores = jnp.where(live_mask, scores, -jnp.inf)
    row_top = jnp.max(scores, axis=-1, keepdims=True)
    raised = jnp.exp(scores - row_top)
    soft_weight = (raised / jnp.sum(raised, axis=-1, keepdims=True)).astype(jnp.bfloat16)
    head_out = jnp.einsum(
        "rkgt,rktd->rkgd", soft_weight, cache_values, preferred_element_type=jnp.float32
    )
    return head_out.astype(jnp.bfloat16).reshape(rows, -1)


def nt_dot(left, right):
    return lax.dot_general(
        left, right, (((1,), (1,)), ((), ())), preferred_element_type=jnp.float32
    )


def iota(shape, dim):
    return lax.broadcasted_iota(jnp.int32, shape, dim)


def one_hot(condition):
    return jnp.where(condition, 1.0, 0.0).astype(jnp.bfloat16)


def routing_kernel(me_ref, ids_ref, gates_ref, owners_ref, table_ref, weight_ref, swap_ref, slot_ref):
    top_count, rows = ids_ref.shape
    experts = owners_ref.shape[1]
    me = me_ref[0]
    ids = ids_ref[...]
    owners = owners_ref[...]
    named = jnp.zeros((experts, rows), jnp.float32)
    expert_at = iota((experts, rows), 0)
    for k in range(top_count):
        named = jnp.where(ids[k : k + 1, :] == expert_at, 1.0, named)
    holds = one_hot(owners == iota((PLANE, experts), 0) + me // PLANE * PLANE)
    routed = jnp.dot(holds, named.astype(jnp.bfloat16), preferred_element_type=jnp.float32)
    earlier = one_hot(iota((rows, rows), 0) < iota((rows, rows), 1))
    before = jnp.dot(routed.astype(jnp.bfloat16), earlier, preferred_element_type=jnp.float32)
    slots = jnp.where(routed > 0.5, before, -1.0)
    slot_ref[...] = slots

    mine = jnp.sum(
        jnp.where(owners == me, iota(owners.shape, 1), 0), axis=1, keepdims=True
    )
    row_gate = jnp.sum(jnp.where(ids == mine, gates_ref[...], 0.0), axis=0, keepdims=True)
    row_slot = jnp.sum(
        jnp.where(iota(slots.shape, 0) == me % PLANE, slots, 0.0), axis=0, keepdims=True
    )
    place = iota((CAP, rows), 0).astype(jnp.float32)
    weight_ref[...] = jnp.sum(jnp.where(row_slot == place, row_gate, 0.0), axis=1, keepdims=True)

    lanes = swap_ref.shape[0]
    source = iota((lanes, lanes), 0)
    target = iota((lanes, lanes), 1)
    swapped = target % 32 + target // 128 * 32 + target // 32 % 4 * 128
    swap_ref[...] = one_hot(source == swapped)

    for holder in range(PLANE):
        table_ref[holder * CAP : (holder + 1) * CAP, :] = one_hot(
            slot_ref[holder : holder + 1, :] == place
        )


def routing(expert_ids, gate_weights, owners, me):
    rows, top_count = expert_ids.shape
    vmem = pl.BlockSpec(memory_space=pltpu.VMEM)
    return pl.pallas_call(
        routing_kernel,
        out_shape=(
            jax.ShapeDtypeStruct((PLANE * CAP, rows), jnp.bfloat16),
            jax.ShapeDtypeStruct((CAP, 1), jnp.float32),
            jax.ShapeDtypeStruct((512, 512), jnp.bfloat16),
        ),
        in_specs=[pl.BlockSpec(memory_space=pltpu.SMEM), vmem, vmem, vmem],
        out_specs=(vmem, vmem, vmem),
        scratch_shapes=[pltpu.VMEM((PLANE, rows), jnp.float32)],
        name="routing",
    )(me.reshape(1), expert_ids.T, gate_weights.T, owners.reshape(1, -1))


def dispatch_kernel(me_ref, parts_ref, table_ref, send_ref, base_ref, wide_ref):
    column, cols, rows = parts_ref.shape
    groups = column // PLANES
    own = base_ref.shape[0]
    share = own // groups
    source = iota((rows, rows), 0)
    target = iota((rows, rows), 1)
    half = rows // 2
    order = one_hot(source == target // 2 % 2 * half + target // 4 * 2 + target % 2)
    for plane in range(PLANES):
        stacked = jnp.concatenate(
            [parts_ref[group * PLANES + plane, :own, :] for group in range(groups)], axis=0
        )
        parts = jnp.dot(stacked, order, preferred_element_type=jnp.float32)
        base = jnp.concatenate(
            [parts_ref[group * PLANES + plane, own:, :] for group in range(groups)], axis=0
        ).astype(jnp.float32)
        for group in range(groups):
            base = base + parts[group * own : (group + 1) * own]
        wide_ref[plane * own : (plane + 1) * own, :] = base
    base_ref[...] = wide_ref[pl.ds(pl.multiple_of(me_ref[0] // PLANE * own, own), own), :]
    hidden_in = wide_ref[...].astype(jnp.bfloat16)
    sent = nt_dot(table_ref[...], hidden_in).astype(jnp.bfloat16)
    send_ref[...] = sent.reshape(send_ref.shape)


def dispatch(parts, table, me, own):
    rows = parts.shape[2]
    vmem = pl.BlockSpec(memory_space=pltpu.VMEM)
    return pl.pallas_call(
        dispatch_kernel,
        out_shape=(
            jax.ShapeDtypeStruct((PLANE, CAP, PLANES * own), jnp.bfloat16),
            jax.ShapeDtypeStruct((own, rows), jnp.float32),
        ),
        in_specs=[pl.BlockSpec(memory_space=pltpu.SMEM), vmem, vmem],
        out_specs=(vmem, vmem),
        scratch_shapes=[pltpu.VMEM((PLANES * own, rows), jnp.float32)],
        name="dispatch",
    )(me.reshape(1), parts, table)


def expert_kernel(
    inbound_ref, gain_ref, weight_ref, swap_ref, gate_ref, up_ref, down_ref, send_ref, fold_ref, flat_ref
):
    width = gain_ref.shape[1]
    span = width // PLANES
    tiles = PLANE // 4
    for block in range(PLANE):
        tile, lane = block // 4, block % 4
        fold_ref[tile * CAP : (tile + 1) * CAP, lane * 128 : (lane + 1) * 128] = inbound_ref[block]
    swap = swap_ref[...]
    turned = jnp.dot(fold_ref[...], swap, preferred_element_type=jnp.float32)
    for tile in range(tiles):
        for plane in range(PLANES):
            at = plane * span + tile * 128
            flat_ref[:, at : at + 128] = turned[
                tile * CAP : (tile + 1) * CAP, plane * 128 : (plane + 1) * 128
            ]
    arrived = flat_ref[...]
    square_mean = jnp.sum(arrived * arrived, axis=1, keepdims=True) / width
    normed = (
        arrived * lax.rsqrt(square_mean + epsilon) * gain_ref[...].astype(jnp.float32)
    ).astype(jnp.bfloat16)
    gate_act = nt_dot(normed, gate_ref[...])
    up_act = nt_dot(normed, up_ref[...])
    hidden = (jax.nn.silu(gate_act) * up_act).astype(jnp.bfloat16)
    expert_out = jnp.dot(hidden, down_ref[...], preferred_element_type=jnp.float32)
    weighted = (expert_out * weight_ref[...]).astype(jnp.bfloat16)
    for tile in range(tiles):
        for plane in range(PLANES):
            at = plane * span + tile * 128
            fold_ref[tile * CAP : (tile + 1) * CAP, plane * 128 : (plane + 1) * 128] = weighted[
                :, at : at + 128
            ]
    back = jnp.dot(fold_ref[...], swap, preferred_element_type=jnp.float32).astype(jnp.bfloat16)
    for block in range(PLANE):
        tile, lane = block // 4, block % 4
        send_ref[block] = back[tile * CAP : (tile + 1) * CAP, lane * 128 : (lane + 1) * 128]


def expert_layer(inbound, norm_gain, weight, swap, gate_proj, up_proj, down_proj):
    width = norm_gain.shape[0]
    vmem = pl.BlockSpec(memory_space=pltpu.VMEM)
    return pl.pallas_call(
        expert_kernel,
        out_shape=jax.ShapeDtypeStruct(inbound.shape, jnp.bfloat16),
        in_specs=[vmem] * 7,
        out_specs=vmem,
        scratch_shapes=[
            pltpu.VMEM((PLANE // 4 * CAP, 512), jnp.bfloat16),
            pltpu.VMEM((CAP, width), jnp.float32),
        ],
        name="expert_layer",
    )(inbound, norm_gain.reshape(1, -1), weight, swap, gate_proj, up_proj, down_proj)


def combine_kernel(returned_ref, table_ref, parts_ref):
    column, cols, rows = parts_ref.shape
    returned = returned_ref[...].reshape(PLANE * CAP, PLANES * cols)
    moe = lax.dot_general(
        returned, table_ref[...], (((0,), (0,)), ((), ())), preferred_element_type=jnp.float32
    ).astype(jnp.bfloat16)
    for at in range(column):
        plane = at % PLANES
        parts_ref[at] = moe[plane * cols : (plane + 1) * cols]


def combine(returned, table, column, cols, rows):
    vmem = pl.BlockSpec(memory_space=pltpu.VMEM)
    return pl.pallas_call(
        combine_kernel,
        out_shape=jax.ShapeDtypeStruct((column, cols, rows), jnp.bfloat16),
        in_specs=[vmem] * 2,
        out_specs=vmem,
        name="combine",
    )(returned, table)


def shards(
    queries,
    cache_keys,
    cache_values,
    lengths,
    out_proj,
    residual,
    norm_gain,
    expert_ids,
    gate_weights,
    owners,
    gate_proj,
    up_proj,
    down_proj,
):
    rows, cols = residual.shape
    groups = lax.axis_size("sec")
    devices = lax.axis_size("dev")
    chips = devices // 2
    me = lax.axis_index("dev")
    table, weight, swap = routing(expert_ids, gate_weights, owners, me)

    head_out = attend(queries, cache_keys, cache_values, lengths)
    same_core = [[2 * chip + core for chip in range(chips)] for core in range(2)]
    swap_core = [(device, device ^ 1) for device in range(devices)]
    gathered = lax.all_to_all(
        jnp.broadcast_to(head_out[None], (chips,) + head_out.shape),
        "dev",
        0,
        0,
        tiled=True,
        axis_index_groups=same_core,
    )
    gathered = gathered.reshape(-1, head_out.shape[1])
    other = lax.ppermute(gathered, "dev", swap_core)
    own_part = nt_dot(out_proj, gathered).astype(jnp.bfloat16)
    other_part = nt_dot(out_proj, other).astype(jnp.bfloat16)
    first = me % 2 == 0
    part = jnp.concatenate(
        [jnp.where(first, own_part, other_part), jnp.where(first, other_part, own_part)], axis=1
    )
    share = cols // groups
    mine = lax.dynamic_slice_in_dim(residual.T, lax.axis_index("sec") * share, share, 0)
    block = jnp.concatenate([part, mine], axis=0)
    column = groups * PLANES
    columns = [
        [group * devices + plane * PLANE + at for group in range(groups) for plane in range(PLANES)]
        for at in range(PLANE)
    ]
    planes = [[plane * PLANE + at for at in range(PLANE)] for plane in range(PLANES)]
    block, table, weight, swap = lax.optimization_barrier((block, table, weight, swap))
    parts = lax.all_to_all(
        jnp.broadcast_to(block[None], (column,) + block.shape),
        ("sec", "dev"),
        0,
        0,
        tiled=True,
        axis_index_groups=columns,
    )
    outbound, base = dispatch(parts, table, me, cols)
    inbound = lax.all_to_all(outbound, "dev", 0, 0, tiled=True, axis_index_groups=planes)
    weighted = expert_layer(
        inbound, norm_gain, weight, swap, gate_proj[0], up_proj[0], down_proj[0]
    )
    returned = lax.all_to_all(weighted, "dev", 0, 0, tiled=True, axis_index_groups=planes)
    moe_parts = lax.all_to_all(
        combine(returned, table, column, cols, rows),
        ("sec", "dev"),
        0,
        0,
        tiled=True,
        axis_index_groups=columns,
    )
    moe = jnp.sum(moe_parts.astype(jnp.float32), axis=0)
    return (base + moe).astype(jnp.bfloat16).T


def solution(mesh):
    in_specs = (
        P("dev", "sec"),
        P("dev", "sec", None, None),
        P("dev", "sec", None, None),
        P("dev"),
        P("dev", "sec"),
        P(None, "dev"),
        P(),
        P(),
        P(),
        P(),
        P("dev", "sec", None),
        P("dev", "sec", None),
        P("dev", "sec", None),
    )
    out_specs = P(None, "dev")
    return jax.shard_map(shards, mesh=mesh, in_specs=in_specs, out_specs=out_specs, check_vma=False)
```

time: 147 us -> 139 us (0.946)
  the two profiles are of different devices: /device:TPU:1 before, /device:TPU:32 now
where the time goes in v2:
time: 139 us; the launch traced here: 138 us
  blocking collectives  103 us (74%)
  Pallas kernels  12.8 us (9%)
  waiting for transfers between devices  9.58 us (7%)
  starting transfers between devices  5.8 us (4%)
  matrix products  2.78 us (2%)
  local copies, waits for them, and re-layouts  2.77 us (2%)
  other arithmetic  1.43 us (1%)
    all_to_all x1, blocking collectives, shards(): lax.all_to_all(jnp.broadcast_to(block[None], (column,) + block.shape), ('...  35.4 us
    all_to_all x1, blocking collectives, shards(): lax.all_to_all(jnp.broadcast_to(head_out[None], (chips,) + head_out.shape...  27.4 us
    all_to_all x1, blocking collectives, shards(): lax.all_to_all(combine(returned, table, column, cols, rows), ('sec', 'dev...  25.5 us
    all_to_all x1, blocking collectives, shards(): lax.all_to_all(weighted, 'dev', 0, 0, tiled=True, axis_index_groups=planes)  14.9 us
    all_to_all x1, waiting for transfers between devices, shards(): lax.all_to_all(outbound, 'dev', 0, 0, tiled=True, axis_index_groups=planes)  9.56 us
    pallas_call x1, Pallas kernels, expert_layer(): pl.pallas_call(expert_kernel, out_shape=jax.ShapeDtypeStruct(inbound.shap...  5.65 us
    all_to_all x1, starting transfers between devices, shards(): lax.all_to_all(outbound, 'dev', 0, 0, tiled=True, axis_index_groups=planes)  3.88 us
  transfers between devices with their start and end apart: 2, of which 1 were waited for; matrix products, arithmetic and copies ran while one was open for 1% of the time, Pallas kernels for 2%

profile of v2, /device:TPU:32, one launch (start us, length us, event | category | flops | bytes accessed | tf_op | source)
XLA Modules:
  0.0 138.4 jit_solution(8228423065246303425)
XLA Ops:
  0.0 0.0 copy-start
  0.0 0.8 iota_compare_fusion
  0.8 0.2 copy-done
  1.0 1.0 fusion.11
  2.0 0.0 copy-start.2
  2.0 1.2 fusion.4
  3.2 0.3 broadcast_in_dim.32
  3.5 27.4 %all_to_all.25 = bf16[64,2,2048]{2,1,0:T(2,128)(2,1)S(1)} all-to-all(bf16[64,2,2048]{2,1,0:T(2,128)(2,1)S(1)} %broadcast_in_dim.32), channel_id=1, replica_groups={{0,2,4,6,8,10,12,14,16,18,20,22,24,26,28,30,32,34,36,38,40,42,44,46,48,..., dimensions={0} | all-to-all | bytes 1048576 | tf_op jit(solution)/shard_map/all_to_all | solution.py:251
  30.9 0.2 reshape.75
  31.1 1.9 %collective-permute-start = (bf16[128,2048]{1,0:T(8,128)(2,1)S(1)}, bf16[128,2048]{1,0:T(8,128)(2,1)S(1)}, u32[]{:S(2)}, u32[]{:S(2)}) collective-permute-start(bf16[128,2048]{1,0:T(8,128)(2,1)S(1)} %reshape.75), channel_id=1, source_target_pairs={{0,1},{1,0},{2,3},{3,2},{4,5},{5,4},{6,7},{7,6},{8,9},{9,8},{10,11... | collective-permute-start | bytes 1572872 | tf_op jit(solution)/shard_map/ppermute | solution.py:260
  33.0 2.3 %routing.1 = (bf16[1536,256]{1,0:T(8,128)(2,1)}, f32[48,1]{1,0:T(8,128)}, bf16[512,512]{1,0:T(8,128)(2,1)}) custom-call(s32[1]{0:T(128)} %bitcast.me_ref, s32[8,256]{1,0:T(8,128)} %bitcast.42, f32[8,256]{1,0:T(8,128)} %bitcast.43, s32[1,128]{1,0:T(1,128)} %bitcast.45), custom_call_target="tpu_custom_call" | custom-call | tf_op jit(solution)/shard_map/routing/pallas_call | solution.py:93
  35.3 0.7 dynamic-slice_bitcast_fusion
  36.0 0.0 copy-done.2
  36.0 0.3 convolution_convert_fusion.1
  36.3 0.0 collective-permute-done
  36.3 0.3 select_bitcast_fusion.1
  36.6 0.0 copy-start.4
  36.6 35.4 %all_to_all.26.parts_ref = bf16[16,40,256]{2,1,0:T(8,128)(2,1)} all-to-all(bf16[16,40,256]{2,1,0:T(8,128)(2,1)S(1)} %broadcast_in_dim.33), channel_id=1, replica_groups={{0,32,64,96,128,160,192,224,256,288,320,352,384,416,448,480},{1,33,65,9..., dimensions={0} | all-to-all | bytes 655360 | tf_op jit(solution)/shard_map/all_to_all | solution.py:277
  72.0 2.6 %dispatch.1 = (bf16[32,48,128]{2,1,0:T(8,128)(2,1)}, f32[32,256]{1,0:T(8,128)}) custom-call(s32[1]{0:T(128)} %bitcast.me_ref, bf16[16,40,256]{2,1,0:T(8,128)(2,1)} %all_to_all.26.parts_ref, bf16[1536,256]{1,0:T(8,128)(2,1)} %get-tuple-element.18.table_ref), custom_call_target="tpu_custom_call" | custom-call | tf_op jit(solution)/shard_map/dispatch/pallas_call | solution.py:136
  74.6 3.9 %all-to-all-start.2 = ((bf16[32,48,128]{2,1,0:T(8,128)(2,1)}), bf16[32,48,128]{2,1,0:T(8,128)(2,1)S(1)}, u32[]{:S(2)}, u32[]{:S(2)}) async-start(bf16[32,48,128]{2,1,0:T(8,128)(2,1)} %get-tuple-element.20), calls=%async_computation.2 | async-start | bytes 786432 | tf_op jit(solution)/shard_map/all_to_all | solution.py:286
  78.5 0.0 copy-done.4
  78.5 0.6 reshape.77.gain_ref
  79.1 9.6 %all-to-all-done.2.inbound_ref = bf16[32,48,128]{2,1,0:T(8,128)(2,1)S(1)} async-done(((bf16[32,48,128]{2,1,0:T(8,128)(2,1)}), bf16[32,48,128]{2,1,0:T(8,128)(2,1)S(1)}, u32[]{:S(2)}, u32[]{:S(2)}) %all-to-all-start.2) | async-done | bytes 393248 | tf_op jit(solution)/shard_map/all_to_all | solution.py:286
  88.7 0.0 copy-start.1
  88.7 0.7 copy-done.1
  89.4 5.6 %expert_layer.1 = bf16[32,48,128]{2,1,0:T(8,128)(2,1)} custom-call(bf16[32,48,128]{2,1,0:T(8,128)(2,1)} %copy-done.1, bf16[1,4096]{1,0:T(2,128)(2,1)} %reshape.77.gain_ref, f32[48,1]{1,0:T(8,128)} %get-tuple-element.21.weight_ref, bf16[512,512]{1,0:T(8,128)(2,1)} %get-tuple-element.22.swap_ref, bf16[192,4096]{1,0:T(8,128)(2,1)} %bitcast.38, ...), custom_call_target="tpu_custom_call" | custom-call | tf_op jit(solution)/shard_map/expert_layer/pallas_call | solution.py:191
  95.1 0.0 copy-start.3
  95.1 14.9 %all_to_all.27.returned_ref = bf16[32,48,128]{2,1,0:T(8,128)(2,1)} all-to-all(bf16[32,48,128]{2,1,0:T(8,128)(2,1)} %expert_layer.1), channel_id=1, replica_groups={{0,1,2,3,4,5,6,7,8,9,10,11,12,13,14,15,16,17,18,19,20,21,22,23,24,25,26..., dimensions={0} | all-to-all | bytes 786432 | tf_op jit(solution)/shard_map/all_to_all | solution.py:290
  110.0 2.3 %combine.1 = bf16[16,32,256]{2,1,0:T(8,128)(2,1)} custom-call(bf16[32,48,128]{2,1,0:T(8,128)(2,1)} %all_to_all.27.returned_ref, bf16[1536,256]{1,0:T(8,128)(2,1)} %get-tuple-element.18.table_ref), custom_call_target="tpu_custom_call" | custom-call | tf_op jit(solution)/shard_map/combine/pallas_call | solution.py:217
  112.2 25.5 %all_to_all.28 = bf16[16,32,256]{2,1,0:T(8,128)(2,1)S(1)} all-to-all(bf16[16,32,256]{2,1,0:T(8,128)(2,1)} %combine.1), channel_id=1, replica_groups={{0,32,64,96,128,160,192,224,256,288,320,352,384,416,448,480},{1,33,65,9..., dimensions={0} | all-to-all | bytes 524288 | tf_op jit(solution)/shard_map/all_to_all | solution.py:291
  137.8 0.0 copy-done.3
  137.8 0.6 fusion.8
  (4 shorter events, 0.1 us)
Async XLA Ops:
  0.0 1.0 copy-start
  2.0 34.0 %copy-start.2 = (bf16[32,2048]{1,0:T(8,128)(2,1)S(1)}, bf16[32,2048]{1,0:T(8,128)(2,1)}, u32[]{:S(2)}) copy-start(bf16[32,2048]{1,0:T(8,128)(2,1)} %param.17) | copy-start | bytes 393220
  31.1 5.2 %collective-permute-start = (bf16[128,2048]{1,0:T(8,128)(2,1)S(1)}, bf16[128,2048]{1,0:T(8,128)(2,1)S(1)}, u32[]{:S(2)}, u32[]{:S(2)}) collective-permute-start(bf16[128,2048]{1,0:T(8,128)(2,1)S(1)} %reshape.75), channel_id=1, source_target_pairs={{0,1},{1,0},{2,3},{3,2},{4,5},{5,4},{6,7},{7,6},{8,9},{9,8},{10,11... | collective-permute-start | bytes 1572872 | tf_op jit(solution)/shard_map/ppermute | solution.py:260
  36.6 41.9 %copy-start.4 = (bf16[4096]{0:T(1024)(128)(2,1)S(1)}, bf16[4096]{0:T(1024)(128)(2,1)}, u32[]{:S(2)}) copy-start(bf16[4096]{0:T(1024)(128)(2,1)} %param.19) | copy-start | bytes 24580
  74.6 14.1 %all-to-all-start.2 = ((bf16[32,48,128]{2,1,0:T(8,128)(2,1)}), bf16[32,48,128]{2,1,0:T(8,128)(2,1)S(1)}, u32[]{:S(2)}, u32[]{:S(2)}) async-start(bf16[32,48,128]{2,1,0:T(8,128)(2,1)} %get-tuple-element.20), calls=%async_computation.2 | async-start | bytes 786432 | tf_op jit(solution)/shard_map/all_to_all | solution.py:286
  88.7 0.7 copy-start.1
  95.1 42.7 %copy-start.3 = (f32[32,256]{1,0:T(8,128)S(1)}, f32[32,256]{1,0:T(8,128)}, u32[]{:S(2)}) copy-start(f32[32,256]{1,0:T(8,128)} %get-tuple-element.19) | copy-start | bytes 98308

commit v3 on v1

v3 whole, which is shorter than its diff:
```python
import functools
import math

import jax
import jax.numpy as jnp
from jax import lax
from jax.experimental import pallas as pl
from jax.experimental.pallas import tpu as pltpu
from jax.sharding import PartitionSpec as P

epsilon = 1e-05

HALF = 64
BANDS = 2
PART = 24
ROW = 32


def attend(queries, cache_keys, cache_values, lengths):
    rows, kv_heads, key_span, head_dim = cache_keys.shape
    group_size = queries.shape[1] // (kv_heads * head_dim)
    grouped = queries.reshape(rows, kv_heads, group_size, head_dim)
    scores = jnp.einsum(
        "rkgd,rktd->rkgt", grouped, cache_keys, preferred_element_type=jnp.float32
    ) / math.sqrt(head_dim)
    live_mask = (
        jnp.arange(key_span, dtype=jnp.int32)[None, None, None, :] < lengths[:, None, None, None]
    )
    scores = jnp.where(live_mask, scores, -jnp.inf)
    row_top = jnp.max(scores, axis=-1, keepdims=True)
    raised = jnp.exp(scores - row_top)
    soft_weight = (raised / jnp.sum(raised, axis=-1, keepdims=True)).astype(jnp.bfloat16)
    head_out = jnp.einsum(
        "rkgt,rktd->rkgd", soft_weight, cache_values, preferred_element_type=jnp.float32
    )
    return head_out.astype(jnp.bfloat16).reshape(rows, -1)


def nt_dot(left, right):
    return lax.dot_general(
        left, right, (((1,), (1,)), ((), ())), preferred_element_type=jnp.float32
    )


def iota(shape, dim):
    return lax.broadcasted_iota(jnp.int32, shape, dim)


def one_hot(condition):
    return jnp.where(condition, 1.0, 0.0).astype(jnp.bfloat16)


def routing_kernel(me_ref, ids_ref, gates_ref, owners_ref, table_ref, weight_ref, swap_ref, slot_ref):
    top_count, rows = ids_ref.shape
    experts = owners_ref.shape[1]
    me = me_ref[0]
    ids = ids_ref[...]
    owners = owners_ref[...]
    named = jnp.zeros((experts, rows), jnp.float32)
    expert_at = iota((experts, rows), 0)
    for k in range(top_count):
        named = jnp.where(ids[k : k + 1, :] == expert_at, 1.0, named)
    holds = one_hot(owners == iota((HALF, experts), 0) + me // HALF * HALF)
    routed = jnp.dot(holds, named.astype(jnp.bfloat16), preferred_element_type=jnp.float32)
    earlier = one_hot(iota((rows, rows), 0) < iota((rows, rows), 1))
    before = jnp.dot(routed.astype(jnp.bfloat16), earlier, preferred_element_type=jnp.float32)
    slots = jnp.where(routed > 0.5, before, -1.0)
    slot_ref[...] = slots

    mine = jnp.sum(
        jnp.where(owners == me, iota(owners.shape, 1), 0), axis=1, keepdims=True
    )
    row_gate = jnp.sum(jnp.where(ids == mine, gates_ref[...], 0.0), axis=0, keepdims=True)
    row_slot = jnp.sum(
        jnp.where(iota(slots.shape, 0) == me % HALF, slots, 0.0), axis=0, keepdims=True
    )
    at = iota((BANDS * ROW, rows), 0)
    place = jnp.where(at % ROW < PART, at // ROW * PART + at % ROW, 4 * rows).astype(jnp.float32)
    weight_ref[...] = jnp.sum(jnp.where(row_slot == place, row_gate, 0.0), axis=1, keepdims=True)

    lanes = swap_ref.shape[0]
    source = iota((lanes, lanes), 0)
    target = iota((lanes, lanes), 1)
    swapped = target % 32 + target // 128 * 32 + target // 32 % 4 * 128
    swap_ref[...] = one_hot(source == swapped)

    for holder in range(HALF):
        for band in range(BANDS):
            table_ref[holder * ROW : (holder + 1) * ROW, band * rows : (band + 1) * rows] = one_hot(
                slot_ref[holder : holder + 1, :] == place[band * ROW : (band + 1) * ROW]
            )


def routing(expert_ids, gate_weights, owners, me):
    rows, top_count = expert_ids.shape
    vmem = pl.BlockSpec(memory_space=pltpu.VMEM)
    return pl.pallas_call(
        routing_kernel,
        out_shape=(
            jax.ShapeDtypeStruct((HALF * ROW, BANDS * rows), jnp.bfloat16),
            jax.ShapeDtypeStruct((BANDS * ROW, 1), jnp.float32),
            jax.ShapeDtypeStruct((512, 512), jnp.bfloat16),
        ),
        in_specs=[pl.BlockSpec(memory_space=pltpu.SMEM), vmem, vmem, vmem],
        out_specs=(vmem, vmem, vmem),
        scratch_shapes=[pltpu.VMEM((HALF, rows), jnp.float32)],
        name="routing",
    )(me.reshape(1), expert_ids.T, gate_weights.T, owners.reshape(1, -1))


def project_kernel(me_ref, heads_ref, own_ref, other_ref, residual_ref, parts_ref, part_ref, *, groups):
    own = own_ref.shape[0]
    span = heads_ref.shape[0]
    width = own_ref.shape[1]
    half = me_ref[0] // HALF
    heads = heads_ref[...]
    scale = 1.0 / groups
    start = pl.multiple_of(half * span, span)
    mine = nt_dot(own_ref[...], heads)
    mine = mine + residual_ref[:, pl.ds(start, span)].astype(jnp.float32) * scale
    theirs = nt_dot(other_ref[:, :width], heads)
    theirs = theirs + other_ref[:, width:].astype(jnp.float32) * scale
    part_ref[pl.ds(pl.multiple_of(half * own, own), own), :] = mine
    part_ref[pl.ds(pl.multiple_of((1 - half) * own, own), own), :] = theirs
    part = part_ref[...].astype(jnp.bfloat16)
    for at in range(parts_ref.shape[0]):
        parts_ref[at] = part


def project(heads, own, other, residual, me, groups):
    span = heads.shape[0]
    cols = own.shape[0]
    vmem = pl.BlockSpec(memory_space=pltpu.VMEM)
    return pl.pallas_call(
        functools.partial(project_kernel, groups=groups),
        out_shape=jax.ShapeDtypeStruct((groups * 2, 2 * cols, span), jnp.bfloat16),
        in_specs=[pl.BlockSpec(memory_space=pltpu.SMEM)] + [vmem] * 4,
        out_specs=vmem,
        scratch_shapes=[pltpu.VMEM((2 * cols, span), jnp.float32)],
        name="project",
    )(me.reshape(1), heads, own, other, residual)


def dispatch_kernel(me_ref, parts_ref, table_ref, send_ref, base_ref, sum_ref, wide_ref):
    column, cols, span = parts_ref.shape
    rows = 2 * span
    own = base_ref.shape[0]
    for half in range(2):
        total = parts_ref[half].astype(jnp.float32)
        for group in range(1, column // 2):
            total = total + parts_ref[group * 2 + half].astype(jnp.float32)
        sum_ref[:, half * span : (half + 1) * span] = total
    base_ref[...] = sum_ref[pl.ds(pl.multiple_of(me_ref[0] // HALF * own, own), own), :]
    hidden_in = sum_ref[...].astype(jnp.bfloat16)
    wide_ref[...] = jnp.zeros(wide_ref.shape, jnp.bfloat16)
    for band in range(BANDS):
        wide_ref[band * cols : (band + 1) * cols, band * rows : (band + 1) * rows] = hidden_in
    sent = nt_dot(table_ref[...], wide_ref[...]).astype(jnp.bfloat16)
    send_ref[...] = sent.reshape(HALF, ROW, BANDS * cols)[:, :PART, :]


def dispatch(parts, table, me):
    cols = parts.shape[1]
    rows = 2 * parts.shape[2]
    vmem = pl.BlockSpec(memory_space=pltpu.VMEM)
    return pl.pallas_call(
        dispatch_kernel,
        out_shape=(
            jax.ShapeDtypeStruct((HALF, PART, BANDS * cols), jnp.bfloat16),
            jax.ShapeDtypeStruct((cols // 2, rows), jnp.float32),
        ),
        in_specs=[pl.BlockSpec(memory_space=pltpu.SMEM), vmem, vmem],
        out_specs=(vmem, vmem),
        scratch_shapes=[
            pltpu.VMEM((cols, rows), jnp.float32),
            pltpu.VMEM((BANDS * cols, BANDS * rows), jnp.bfloat16),
        ],
        name="dispatch",
    )(me.reshape(1), parts, table)


def expert_kernel(
    inbound_ref, gain_ref, weight_ref, swap_ref, gate_ref, up_ref, down_ref, send_ref, fold_ref, flat_ref
):
    width = gain_ref.shape[1]
    pieces = []
    for tile in range(HALF // 4):
        for band in range(BANDS):
            for high in range(2):
                at = (tile // 8 + 2 * high) * (width // 4) + tile % 8 * 128
                pieces.append((tile * ROW, band * 2 + high, band * ROW, at))
    fold_ref[...] = jnp.zeros(fold_ref.shape, fold_ref.dtype)
    for block in range(HALF):
        tile, lane = block // 4, block % 4
        fold_ref[tile * ROW : tile * ROW + PART, lane * 128 : (lane + 1) * 128] = inbound_ref[block]
    swap = swap_ref[...]
    turned = jnp.dot(fold_ref[...], swap, preferred_element_type=jnp.float32)
    for row, lane, place, at in pieces:
        flat_ref[place : place + ROW, at : at + 128] = turned[
            row : row + ROW, lane * 128 : (lane + 1) * 128
        ]
    arrived = flat_ref[...]
    square_mean = jnp.sum(arrived * arrived, axis=1, keepdims=True) / width
    normed = (
        arrived * lax.rsqrt(square_mean + epsilon) * gain_ref[...].astype(jnp.float32)
    ).astype(jnp.bfloat16)
    gate_act = nt_dot(normed, gate_ref[...])
    up_act = nt_dot(normed, up_ref[...])
    hidden = (jax.nn.silu(gate_act) * up_act).astype(jnp.bfloat16)
    expert_out = jnp.dot(hidden, down_ref[...], preferred_element_type=jnp.float32)
    weighted = (expert_out * weight_ref[...]).astype(jnp.bfloat16)
    for row, lane, place, at in pieces:
        fold_ref[row : row + ROW, lane * 128 : (lane + 1) * 128] = weighted[
            place : place + ROW, at : at + 128
        ]
    back = jnp.dot(fold_ref[...], swap, preferred_element_type=jnp.float32).astype(jnp.bfloat16)
    for block in range(HALF):
        tile, lane = block // 4, block % 4
        send_ref[block] = back[tile * ROW : tile * ROW + PART, lane * 128 : (lane + 1) * 128]


def expert_layer(inbound, norm_gain, weight, swap, gate_proj, up_proj, down_proj):
    width = norm_gain.shape[0]
    vmem = pl.BlockSpec(memory_space=pltpu.VMEM)
    return pl.pallas_call(
        expert_kernel,
        out_shape=jax.ShapeDtypeStruct(inbound.shape, jnp.bfloat16),
        in_specs=[vmem] * 7,
        out_specs=vmem,
        scratch_shapes=[
            pltpu.VMEM((HALF // 4 * ROW, 512), jnp.bfloat16),
            pltpu.VMEM((BANDS * ROW, width), jnp.float32),
        ],
        name="expert_layer",
    )(inbound, norm_gain.reshape(1, -1), weight, swap, gate_proj, up_proj, down_proj)


def combine_kernel(returned_ref, table_ref, parts_ref, rows_ref):
    column, own, rows = parts_ref.shape
    cols = 2 * own
    rows_ref[...] = jnp.zeros(rows_ref.shape, rows_ref.dtype)
    for block in range(HALF):
        rows_ref[block * ROW : block * ROW + PART, :] = returned_ref[block]
    mixed = lax.dot_general(
        rows_ref[...], table_ref[...], (((0,), (0,)), ((), ())), preferred_element_type=jnp.float32
    )
    moe = (mixed[:cols, :rows] + mixed[cols:, rows:]).astype(jnp.bfloat16)
    for at in range(column):
        parts_ref[at] = moe[at % 2 * own : (at % 2 + 1) * own]


def combine(returned, table, column, own, rows):
    vmem = pl.BlockSpec(memory_space=pltpu.VMEM)
    return pl.pallas_call(
        combine_kernel,
        out_shape=jax.ShapeDtypeStruct((column, own, rows), jnp.bfloat16),
        in_specs=[vmem] * 2,
        out_specs=vmem,
        scratch_shapes=[pltpu.VMEM((HALF * ROW, 2 * BANDS * own), jnp.bfloat16)],
        name="combine",
    )(returned, table)


def shards(
    queries,
    cache_keys,
    cache_values,
    lengths,
    out_proj,
    residual,
    norm_gain,
    expert_ids,
    gate_weights,
    owners,
    gate_proj,
    up_proj,
    down_proj,
):
    rows, cols = residual.shape
    groups = lax.axis_size("sec")
    devices = lax.axis_size("dev")
    column = groups * 2
    me = lax.axis_index("dev")
    halves = [[half * HALF + at for at in range(HALF)] for half in range(2)]
    columns = [
        [group * devices + half * HALF + at for group in range(groups) for half in range(2)]
        for at in range(HALF)
    ]

    def over(x, axis, groups_of):
        return lax.all_to_all(x, axis, 0, 0, tiled=True, axis_index_groups=groups_of)

    facing = [(device, device ^ HALF) for device in range(devices)]
    residual = residual.T
    half_rows = rows // 2
    wanted = lax.dynamic_slice_in_dim(residual, (1 - me // HALF) * half_rows, half_rows, 1)
    other = lax.ppermute(jnp.concatenate([out_proj, wanted], axis=1), "dev", facing)

    head_out = attend(queries, cache_keys, cache_values, lengths)
    head_out, expert_ids = lax.optimization_barrier((head_out, expert_ids))
    table, weight, swap = routing(expert_ids, gate_weights, owners, me)
    heads = over(jnp.broadcast_to(head_out[None], (HALF,) + head_out.shape), "dev", halves)
    parts = project(heads.reshape(half_rows, -1), out_proj, other, residual, me, groups)
    parts, table, weight, swap = lax.optimization_barrier((parts, table, weight, swap))
    parts = over(parts, ("sec", "dev"), columns)
    outbound, base = dispatch(parts, table, me)
    inbound = over(outbound, "dev", halves)
    weighted = expert_layer(
        inbound, norm_gain, weight, swap, gate_proj[0], up_proj[0], down_proj[0]
    )
    returned = over(weighted, "dev", halves)
    moe_parts = over(combine(returned, table, column, cols, rows), ("sec", "dev"), columns)
    moe = jnp.sum(moe_parts.astype(jnp.float32), axis=0)
    return (base + moe).astype(jnp.bfloat16).T


def solution(mesh):
    in_specs = (
        P("dev", "sec"),
        P("dev", "sec", None, None),
        P("dev", "sec", None, None),
        P("dev"),
        P("dev", "sec"),
        P(None, "dev"),
        P(),
        P(),
        P(),
        P(),
        P("dev", "sec", None),
        P("dev", "sec", None),
        P("dev", "sec", None),
    )
    out_specs = P(None, "dev")
    return jax.shard_map(shards, mesh=mesh, in_specs=in_specs, out_specs=out_specs, check_vma=False)
```

time: 147 us -> 126 us (0.86)
  blocking collectives: 70.6 us -> 59.9 us
  waiting for transfers between devices: 26.1 us -> 18.2 us
  starting transfers between devices: 23.7 us -> 21.8 us
  Pallas kernels: 18.6 us -> 17 us
    all_to_all x3, blocking collectives: 70.6 us -> 59.9 us  [over(): lax.all_to_all(x, axis, 0, 0, tiled=True, axis_index_groups=groups_of)]
    all_to_all x2, waiting for transfers between devices: 24.9 us -> 18.2 us  [over(): lax.all_to_all(x, axis, 0, 0, tiled=True, axis_index_groups=groups_of)]
    all_to_all x2, starting transfers between devices: 19.7 us -> 17.4 us  [over(): lax.all_to_all(x, axis, 0, 0, tiled=True, axis_index_groups=groups_of)]
    pallas_call x3 -> x4, Pallas kernels: 12.8 us -> 11.2 us  [the longest x1 3.17 us: dispatch(): pl.pallas_call(dispatch_kernel, out_shape=(jax.ShapeDtypeStruct((HALF, PA...]
  transfers between devices with their start and end apart: 3 -> 3, of which waited for: 3 -> 2; matrix products, arithmetic and copies ran while one was open for 1% -> 1% of each run, Pallas kernels for 3% -> 2%
where the time goes in v3:
time: 126 us; the launch traced here: 125 us
  blocking collectives  59.9 us (48%)
  starting transfers between devices  21.8 us (17%)
  waiting for transfers between devices  18.2 us (14%)
  Pallas kernels  17 us (13%)
  local copies, waits for them, and re-layouts  4.32 us (3%)
  matrix products  2.2 us (2%)
  other arithmetic  1.42 us (1%)
    all_to_all x3, blocking collectives, over(): lax.all_to_all(x, axis, 0, 0, tiled=True, axis_index_groups=groups_of)  59.9 us
    all_to_all x2, waiting for transfers between devices, over(): lax.all_to_all(x, axis, 0, 0, tiled=True, axis_index_groups=groups_of)  18.2 us
    all_to_all x2, starting transfers between devices, over(): lax.all_to_all(x, axis, 0, 0, tiled=True, axis_index_groups=groups_of)  17.4 us
    pallas_call x1, Pallas kernels, expert_layer(): pl.pallas_call(expert_kernel, out_shape=jax.ShapeDtypeStruct(inbound.shap...  5.79 us
    ppermute x1, starting transfers between devices, shards(): lax.ppermute(jnp.concatenate([out_proj, wanted], axis=1), 'dev', facing)  4.33 us
    pallas_call x1, Pallas kernels, dispatch(): pl.pallas_call(dispatch_kernel, out_shape=(jax.ShapeDtypeStruct((HALF, PA...  3.17 us
    pallas_call x1, Pallas kernels, combine(): pl.pallas_call(combine_kernel, out_shape=jax.ShapeDtypeStruct((column, ow...  2.94 us
    pallas_call x1, Pallas kernels, routing(): pl.pallas_call(routing_kernel, out_shape=(jax.ShapeDtypeStruct((HALF * RO...  2.9 us
  transfers between devices with their start and end apart: 3, of which 2 were waited for; matrix products, arithmetic and copies ran while one was open for 1% of the time, Pallas kernels for 2%

profile of v3, /device:TPU:1, one launch (start us, length us, event | category | flops | bytes accessed | tf_op | source)
XLA Modules:
  0.0 125.1 jit_solution(6294680713850096196)
XLA Ops:
  0.0 0.0 copy-start
  0.0 0.0 copy-start.4
  0.0 0.0 copy-start.2
  0.0 0.8 iota_compare_fusion
  0.8 0.2 copy-done
  1.0 1.0 fusion.11
  2.0 1.2 fusion.4
  3.2 1.1 broadcast_in_dim.24
  4.3 10.9 %all-to-all-start = ((bf16[64,2,2048]{2,1,0:T(2,128)(2,1)}), bf16[64,2,2048]{2,1,0:T(2,128)(2,1)S(1)}, u32[]{:S(2)}, u32[]{:S(2)}) async-start(bf16[64,2,2048]{2,1,0:T(2,128)(2,1)} %broadcast_in_dim.24), calls=%async_computation | async-start | bytes 1048576 | tf_op jit(solution)/shard_map/all_to_all | solution.py:291
  15.2 0.0 copy-done.4
  15.2 0.0 copy-done.2
  15.3 4.3 %collective-permute-start = (bf16[32,2176]{1,0:T(8,128)(2,1)S(1)}, bf16[32,2176]{1,0:T(8,128)(2,1)S(1)}, u32[]{:S(2)}, u32[]{:S(2)}) collective-permute-start(bf16[32,2176]{1,0:T(8,128)(2,1)S(1)} %pad_maximum_fusion), channel_id=1, source_target_pairs={{0,64},{1,65},{2,66},{3,67},{4,68},{5,69},{6,70},{7,71},{8,72},{9,... | collective-permute-start | bytes 417800 | tf_op jit(solution)/shard_map/ppermute | solution.py:297
  19.6 2.9 %routing.1 = (bf16[2048,512]{1,0:T(8,128)(2,1)}, f32[64,1]{1,0:T(8,128)}, bf16[512,512]{1,0:T(8,128)(2,1)}) custom-call(s32[1]{0:T(128)} %bitcast.me_ref, s32[8,256]{1,0:T(8,128)} %bitcast.36, f32[8,256]{1,0:T(8,128)} %bitcast.37, s32[1,128]{1,0:T(1,128)} %bitcast.39), custom_call_target="tpu_custom_call" | custom-call | tf_op jit(solution)/shard_map/routing/pallas_call | solution.py:97
  22.5 7.9 %all-to-all-done = bf16[64,2,2048]{2,1,0:T(2,128)(2,1)S(1)} async-done(((bf16[64,2,2048]{2,1,0:T(2,128)(2,1)}), bf16[64,2,2048]{2,1,0:T(2,128)(2,1)S(1)}, u32[]{:S(2)}, u32[]{:S(2)}) %all-to-all-start) | async-done | bytes 524320 | tf_op jit(solution)/shard_map/all_to_all | solution.py:291
  30.4 1.0 reshape.79.heads_ref
  31.4 0.0 collective-permute-done.other_ref
  31.4 0.0 copy-start.3
  31.4 0.7 copy-done.3
  32.1 2.2 %project.1 = bf16[8,64,128]{2,1,0:T(8,128)(2,1)} custom-call(s32[1]{0:T(128)} %bitcast.me_ref, bf16[128,2048]{1,0:T(8,128)(2,1)} %reshape.79.heads_ref, bf16[32,2048]{1,0:T(8,128)(2,1)} %own_ref.1, bf16[32,2176]{1,0:T(8,128)(2,1)} %copy-done.3, bf16[32,256]{1,0:T(8,128)(2,1)} %bitcast.34), custom_call_target="tpu_custom_call" | custom-call | tf_op jit(solution)/shard_map/project/pallas_call | solution.py:134
  34.3 26.6 %all_to_all.25.parts_ref = bf16[8,64,128]{2,1,0:T(8,128)(2,1)} all-to-all(bf16[8,64,128]{2,1,0:T(8,128)(2,1)} %project.1), channel_id=1, replica_groups={{0,64,128,192,256,320,384,448},{1,65,129,193,257,321,385,449},{2,66,130..., dimensions={0} | all-to-all | bytes 262144 | tf_op jit(solution)/shard_map/all_to_all | solution.py:291
  61.0 0.0 copy-start.6
  61.0 3.2 %dispatch.1 = (bf16[64,24,128]{2,1,0:T(8,128)(2,1)}, f32[32,256]{1,0:T(8,128)}) custom-call(s32[1]{0:T(128)} %bitcast.me_ref, bf16[8,64,128]{2,1,0:T(8,128)(2,1)} %all_to_all.25.parts_ref, bf16[2048,512]{1,0:T(8,128)(2,1)} %get-tuple-element.22.table_ref), custom_call_target="tpu_custom_call" | custom-call | tf_op jit(solution)/shard_map/dispatch/pallas_call | solution.py:166
  64.1 6.5 %all-to-all-start.2 = ((bf16[64,24,128]{2,1,0:T(8,128)(2,1)}), bf16[64,24,128]{2,1,0:T(8,128)(2,1)S(1)}, u32[]{:S(2)}, u32[]{:S(2)}) async-start(bf16[64,24,128]{2,1,0:T(8,128)(2,1)} %get-tuple-element.24), calls=%async_computation.2 | async-start | bytes 786432 | tf_op jit(solution)/shard_map/all_to_all | solution.py:291
  70.7 0.0 copy-done.6
  70.7 0.6 reshape.81.gain_ref
  71.3 10.3 %all-to-all-done.2.inbound_ref = bf16[64,24,128]{2,1,0:T(8,128)(2,1)S(1)} async-done(((bf16[64,24,128]{2,1,0:T(8,128)(2,1)}), bf16[64,24,128]{2,1,0:T(8,128)(2,1)S(1)}, u32[]{:S(2)}, u32[]{:S(2)}) %all-to-all-start.2) | async-done | bytes 393248 | tf_op jit(solution)/shard_map/all_to_all | solution.py:291
  81.6 0.0 copy-start.1
  81.6 0.7 copy-done.1
  82.4 5.8 %expert_layer.1 = bf16[64,24,128]{2,1,0:T(8,128)(2,1)} custom-call(bf16[64,24,128]{2,1,0:T(8,128)(2,1)} %copy-done.1, bf16[1,4096]{1,0:T(2,128)(2,1)} %reshape.81.gain_ref, f32[64,1]{1,0:T(8,128)} %get-tuple-element.25.weight_ref, bf16[512,512]{1,0:T(8,128)(2,1)} %get-tuple-element.26.swap_ref, bf16[192,4096]{1,0:T(8,128)(2,1)} %bitcast.31, ...), custom_call_target="tpu_custom_call" | custom-call | tf_op jit(solution)/shard_map/expert_layer/pallas_call | solution.py:225
  88.2 16.3 %all_to_all.26.returned_ref = bf16[64,24,128]{2,1,0:T(8,128)(2,1)} all-to-all(bf16[64,24,128]{2,1,0:T(8,128)(2,1)} %expert_layer.1), channel_id=1, replica_groups={{0,1,2,3,4,5,6,7,8,9,10,11,12,13,14,15,16,17,18,19,20,21,22,23,24,25,26..., dimensions={0} | all-to-all | bytes 786432 | tf_op jit(solution)/shard_map/all_to_all | solution.py:291
  104.4 0.0 copy-start.5
  104.4 2.9 %combine.1 = bf16[8,32,256]{2,1,0:T(8,128)(2,1)} custom-call(bf16[64,24,128]{2,1,0:T(8,128)(2,1)} %all_to_all.26.returned_ref, bf16[2048,512]{1,0:T(8,128)(2,1)} %get-tuple-element.22.table_ref), custom_call_target="tpu_custom_call" | custom-call | tf_op jit(solution)/shard_map/combine/pallas_call | solution.py:254
  107.4 17.0 %all_to_all.27 = bf16[8,32,256]{2,1,0:T(8,128)(2,1)S(1)} all-to-all(bf16[8,32,256]{2,1,0:T(8,128)(2,1)} %combine.1), channel_id=1, replica_groups={{0,64,128,192,256,320,384,448},{1,65,129,193,257,321,385,449},{2,66,130..., dimensions={0} | all-to-all | bytes 262144 | tf_op jit(solution)/shard_map/all_to_all | solution.py:291
  124.4 0.0 copy-done.5
  124.5 0.6 fusion.8
  (4 shorter events, 0.1 us)
Async XLA Ops:
  0.0 1.0 copy-start
  0.0 15.2 %copy-start.4 = (bf16[256,32]{0,1:T(8,128)(2,1)S(1)}, bf16[256,32]{0,1:T(8,128)(2,1)}, u32[]{:S(2)}) copy-start(bf16[256,32]{0,1:T(8,128)(2,1)} %param.18) | copy-start | bytes 49156
  0.0 15.2 %copy-start.2 = (bf16[32,2048]{1,0:T(8,128)(2,1)S(1)}, bf16[32,2048]{1,0:T(8,128)(2,1)}, u32[]{:S(2)}) copy-start(bf16[32,2048]{1,0:T(8,128)(2,1)} %own_ref.1) | copy-start | bytes 393220
  4.3 26.2 %all-to-all-start = ((bf16[64,2,2048]{2,1,0:T(2,128)(2,1)}), bf16[64,2,2048]{2,1,0:T(2,128)(2,1)S(1)}, u32[]{:S(2)}, u32[]{:S(2)}) async-start(bf16[64,2,2048]{2,1,0:T(2,128)(2,1)} %broadcast_in_dim.24), calls=%async_computation | async-start | bytes 1048576 | tf_op jit(solution)/shard_map/all_to_all | solution.py:291
  15.3 16.2 %collective-permute-start = (bf16[32,2176]{1,0:T(8,128)(2,1)S(1)}, bf16[32,2176]{1,0:T(8,128)(2,1)S(1)}, u32[]{:S(2)}, u32[]{:S(2)}) collective-permute-start(bf16[32,2176]{1,0:T(8,128)(2,1)S(1)} %pad_maximum_fusion), channel_id=1, source_target_pairs={{0,64},{1,65},{2,66},{3,67},{4,68},{5,69},{6,70},{7,71},{8,72},{9,... | collective-permute-start | bytes 417800 | tf_op jit(solution)/shard_map/ppermute | solution.py:297
  31.4 0.7 copy-start.3
  61.0 9.7 %copy-start.6 = (bf16[4096]{0:T(1024)(128)(2,1)S(1)}, bf16[4096]{0:T(1024)(128)(2,1)}, u32[]{:S(2)}) copy-start(bf16[4096]{0:T(1024)(128)(2,1)} %param.19) | copy-start | bytes 24580
  64.1 17.5 %all-to-all-start.2 = ((bf16[64,24,128]{2,1,0:T(8,128)(2,1)}), bf16[64,24,128]{2,1,0:T(8,128)(2,1)S(1)}, u32[]{:S(2)}, u32[]{:S(2)}) async-start(bf16[64,24,128]{2,1,0:T(8,128)(2,1)} %get-tuple-element.24), calls=%async_computation.2 | async-start | bytes 786432 | tf_op jit(solution)/shard_map/all_to_all | solution.py:291
  81.6 0.7 copy-start.1
  104.4 20.0 %copy-start.5 = (f32[32,256]{1,0:T(8,128)S(1)}, f32[32,256]{1,0:T(8,128)}, u32[]{:S(2)}) copy-start(f32[32,256]{1,0:T(8,128)} %get-tuple-element.23) | copy-start | bytes 98308

commit v4 on v3

--- a/solution.py
+++ b/solution.py
@@ -14,26 +14,7 @@
 BANDS = 2
 PART = 24
 ROW = 32
-
-
-def attend(queries, cache_keys, cache_values, lengths):
-    rows, kv_heads, key_span, head_dim = cache_keys.shape
-    group_size = queries.shape[1] // (kv_heads * head_dim)
-    grouped = queries.reshape(rows, kv_heads, group_size, head_dim)
-    scores = jnp.einsum(
-        "rkgd,rktd->rkgt", grouped, cache_keys, preferred_element_type=jnp.float32
-    ) / math.sqrt(head_dim)
-    live_mask = (
-        jnp.arange(key_span, dtype=jnp.int32)[None, None, None, :] < lengths[:, None, None, None]
-    )
-    scores = jnp.where(live_mask, scores, -jnp.inf)
-    row_top = jnp.max(scores, axis=-1, keepdims=True)
-    raised = jnp.exp(scores - row_top)
-    soft_weight = (raised / jnp.sum(raised, axis=-1, keepdims=True)).astype(jnp.bfloat16)
-    head_out = jnp.einsum(
-        "rkgt,rktd->rkgd", soft_weight, cache_values, preferred_element_type=jnp.float32
-    )
-    return head_out.astype(jnp.bfloat16).reshape(rows, -1)
+VMEM_LIMIT = 24 << 20
 
 
 def nt_dot(left, right):
@@ -46,8 +27,83 @@
     return lax.broadcasted_iota(jnp.int32, shape, dim)
 
 
+def near(*arrays):
+    return tuple(pltpu.with_memory_space_constraint(array, pltpu.VMEM) for array in arrays)
+
+
+def far(*arrays):
+    return tuple(pltpu.with_memory_space_constraint(array, pltpu.HBM) for array in arrays)
+
+
 def one_hot(condition):
     return jnp.where(condition, 1.0, 0.0).astype(jnp.bfloat16)
+
+
+def attend_kernel(
+    lengths_ref,
+    queries_hbm,
+    keys_hbm,
+    values_hbm,
+    out_ref,
+    query_ref,
+    queries_ref,
+    keys_ref,
+    values_ref,
+    sems,
+):
+    copies = [
+        pltpu.make_async_copy(source, target, sems.at[at])
+        for at, (source, target) in enumerate(
+            ((queries_hbm, queries_ref), (keys_hbm, keys_ref), (values_hbm, values_ref))
+        )
+    ]
+    for copy in copies:
+        copy.start()
+    rows, _, key_span, head_dim = keys_ref.shape
+    group_size = queries_ref.shape[1] // head_dim
+    position = iota((group_size, key_span), 1)
+    copies[0].wait()
+    queries = queries_ref[...].astype(jnp.float32)
+    outs = []
+    copies[1].wait()
+    for row in range(rows):
+        for head in range(group_size):
+            query_ref[row, head : head + 1, :] = queries[
+                row : row + 1, head * head_dim : (head + 1) * head_dim
+            ]
+        scores = nt_dot(query_ref[row].astype(jnp.bfloat16), keys_ref[row, 0]) / math.sqrt(head_dim)
+        scores = jnp.where(position < lengths_ref[row], scores, -jnp.inf)
+        row_top = jnp.max(scores, axis=-1, keepdims=True)
+        raised = jnp.exp(scores - row_top)
+        soft_weight = (raised / jnp.sum(raised, axis=-1, keepdims=True)).astype(jnp.bfloat16)
+        if row == 0:
+            copies[2].wait()
+        outs.append(jnp.dot(soft_weight, values_ref[row, 0], preferred_element_type=jnp.float32))
+    for head in range(group_size):
+        pair = jnp.concatenate([out[head : head + 1, :] for out in outs], axis=0)
+        out_ref[:, head * head_dim : (head + 1) * head_dim] = pair.astype(jnp.bfloat16)
+
+
+def attend(queries, cache_keys, cache_values, lengths):
+    rows, width = queries.shape
+    head_dim = cache_keys.shape[3]
+    vmem = pl.BlockSpec(memory_space=pltpu.VMEM)
+    return pl.pallas_call(
+        attend_kernel,
+        out_shape=pltpu.VMEM(queries.shape, jnp.bfloat16),
+        in_specs=[pl.BlockSpec(memory_space=pltpu.SMEM)]
+        + [pl.BlockSpec(memory_space=pltpu.HBM)] * 3,
+        out_specs=vmem,
+        scratch_shapes=[
+            pltpu.VMEM((rows, width // head_dim, head_dim), jnp.float32),
+            pltpu.VMEM(queries.shape, jnp.bfloat16),
+            pltpu.VMEM(cache_keys.shape, jnp.bfloat16),
+            pltpu.VMEM(cache_values.shape, jnp.bfloat16),
+            pltpu.SemaphoreType.DMA((3,)),
+        ],
+        name="attend",
+        compiler_params=pltpu.CompilerParams(vmem_limit_bytes=VMEM_LIMIT),
+    )(*far(lengths, queries, cache_keys, cache_values))
 
 
 def routing_kernel(me_ref, ids_ref, gates_ref, owners_ref, table_ref, weight_ref, swap_ref, slot_ref):
@@ -97,15 +153,16 @@
     return pl.pallas_call(
         routing_kernel,
         out_shape=(
-            jax.ShapeDtypeStruct((HALF * ROW, BANDS * rows), jnp.bfloat16),
-            jax.ShapeDtypeStruct((BANDS * ROW, 1), jnp.float32),
-            jax.ShapeDtypeStruct((512, 512), jnp.bfloat16),
+            pltpu.VMEM((HALF * ROW, BANDS * rows), jnp.bfloat16),
+            pltpu.VMEM((BANDS * ROW, 1), jnp.float32),
+            pltpu.VMEM((512, 512), jnp.bfloat16),
         ),
         in_specs=[pl.BlockSpec(memory_space=pltpu.SMEM), vmem, vmem, vmem],
         out_specs=(vmem, vmem, vmem),
         scratch_shapes=[pltpu.VMEM((HALF, rows), jnp.float32)],
         name="routing",
-    )(me.reshape(1), expert_ids.T, gate_weights.T, owners.reshape(1, -1))
+        compiler_params=pltpu.CompilerParams(vmem_limit_bytes=VMEM_LIMIT),
+    )(me.reshape(1), *near(expert_ids.T, gate_weights.T, owners.reshape(1, -1)))
 
 
 def project_kernel(me_ref, heads_ref, own_ref, other_ref, residual_ref, parts_ref, part_ref, *, groups):
@@ -133,12 +190,13 @@
     vmem = pl.BlockSpec(memory_space=pltpu.VMEM)
     return pl.pallas_call(
         functools.partial(project_kernel, groups=groups),
-        out_shape=jax.ShapeDtypeStruct((groups * 2, 2 * cols, span), jnp.bfloat16),
+        out_shape=pltpu.VMEM((groups * 2, 2 * cols, span), jnp.bfloat16),
         in_specs=[pl.BlockSpec(memory_space=pltpu.SMEM)] + [vmem] * 4,
         out_specs=vmem,
         scratch_shapes=[pltpu.VMEM((2 * cols, span), jnp.float32)],
         name="project",
-    )(me.reshape(1), heads, own, other, residual)
+        compiler_params=pltpu.CompilerParams(vmem_limit_bytes=VMEM_LIMIT),
+    )(me.reshape(1), *near(heads, own, other, residual))
 
 
 def dispatch_kernel(me_ref, parts_ref, table_ref, send_ref, base_ref, sum_ref, wide_ref):
@@ -166,8 +224,8 @@
     return pl.pallas_call(
         dispatch_kernel,
         out_shape=(
-            jax.ShapeDtypeStruct((HALF, PART, BANDS * cols), jnp.bfloat16),
-            jax.ShapeDtypeStruct((cols // 2, rows), jnp.float32),
+            pltpu.VMEM((HALF, PART, BANDS * cols), jnp.bfloat16),
+            pltpu.VMEM((cols // 2, rows), jnp.float32),
         ),
         in_specs=[pl.BlockSpec(memory_space=pltpu.SMEM), vmem, vmem],
         out_specs=(vmem, vmem),
@@ -176,12 +234,34 @@
             pltpu.VMEM((BANDS * cols, BANDS * rows), jnp.bfloat16),
         ],
         name="dispatch",
-    )(me.reshape(1), parts, table)
+        compiler_params=pltpu.CompilerParams(vmem_limit_bytes=VMEM_LIMIT),
+    )(me.reshape(1), *near(parts, table))
 
 
 def expert_kernel(
-    inbound_ref, gain_ref, weight_ref, swap_ref, gate_ref, up_ref, down_ref, send_ref, fold_ref, flat_ref
+    inbound_ref,
+    gain_ref,
+    weight_ref,
+    swap_ref,
+    gate_hbm,
+    up_hbm,
+    down_hbm,
+    send_ref,
+    fold_ref,
+    flat_ref,
+    gate_ref,
+    up_ref,
+    down_ref,
+    sems,
 ):
+    copies = [
+        pltpu.make_async_copy(source, target, sems.at[at])
+        for at, (source, target) in enumerate(
+            ((gate_hbm, gate_ref), (up_hbm, up_ref), (down_hbm, down_ref))
+        )
+    ]
+    for copy in copies:
+        copy.start()
     width = gain_ref.shape[1]
     pieces = []
     for tile in range(HALF // 4):
@@ -204,9 +284,12 @@
     normed = (
         arrived * lax.rsqrt(square_mean + epsilon) * gain_ref[...].astype(jnp.float32)
     ).astype(jnp.bfloat16)
+    copies[0].wait()
     gate_act = nt_dot(normed, gate_ref[...])
+    copies[1].wait()
     up_act = nt_dot(normed, up_ref[...])
     hidden = (jax.nn.silu(gate_act) * up_act).astype(jnp.bfloat16)
+    copies[2].wait()
     expert_out = jnp.dot(hidden, down_ref[...], preferred_element_type=jnp.float32)
     weighted = (expert_out * weight_ref[...]).astype(jnp.bfloat16)
     for row, lane, place, at in pieces:
@@ -220,19 +303,24 @@
 
 
 def expert_layer(inbound, norm_gain, weight, swap, gate_proj, up_proj, down_proj):
-    width = norm_gain.shape[0]
+    width = norm_gain.shape[1]
     vmem = pl.BlockSpec(memory_space=pltpu.VMEM)
     return pl.pallas_call(
         expert_kernel,
-        out_shape=jax.ShapeDtypeStruct(inbound.shape, jnp.bfloat16),
-        in_specs=[vmem] * 7,
+        out_shape=pltpu.VMEM(inbound.shape, jnp.bfloat16),
+        in_specs=[vmem] * 4 + [pl.BlockSpec(memory_space=pltpu.HBM)] * 3,
         out_specs=vmem,
         scratch_shapes=[
             pltpu.VMEM((HALF // 4 * ROW, 512), jnp.bfloat16),
             pltpu.VMEM((BANDS * ROW, width), jnp.float32),
+            pltpu.VMEM(gate_proj.shape, jnp.bfloat16),
+            pltpu.VMEM(up_proj.shape, jnp.bfloat16),
+            pltpu.VMEM(down_proj.shape, jnp.bfloat16),
+            pltpu.SemaphoreType.DMA((3,)),
         ],
         name="expert_layer",
-    )(inbound, norm_gain.reshape(1, -1), weight, swap, gate_proj, up_proj, down_proj)
+        compiler_params=pltpu.CompilerParams(vmem_limit_bytes=VMEM_LIMIT),
+    )(*near(inbound, norm_gain, weight, swap), *far(gate_proj, up_proj, down_proj))
 
 
 def combine_kernel(returned_ref, table_ref, parts_ref, rows_ref):
@@ -253,12 +341,13 @@
     vmem = pl.BlockSpec(memory_space=pltpu.VMEM)
     return pl.pallas_call(
         combine_kernel,
-        out_shape=jax.ShapeDtypeStruct((column, own, rows), jnp.bfloat16),
+        out_shape=pltpu.VMEM((column, own, rows), jnp.bfloat16),
         in_specs=[vmem] * 2,
         out_specs=vmem,
         scratch_shapes=[pltpu.VMEM((HALF * ROW, 2 * BANDS * own), jnp.bfloat16)],
         name="combine",
-    )(returned, table)
+        compiler_params=pltpu.CompilerParams(vmem_limit_bytes=VMEM_LIMIT),
+    )(*near(returned, table))
 
 
 def shards(
@@ -301,12 +390,15 @@
     table, weight, swap = routing(expert_ids, gate_weights, owners, me)
     heads = over(jnp.broadcast_to(head_out[None], (HALF,) + head_out.shape), "dev", halves)
     parts = project(heads.reshape(half_rows, -1), out_proj, other, residual, me, groups)
-    parts, table, weight, swap = lax.optimization_barrier((parts, table, weight, swap))
+    gain = norm_gain.reshape(1, -1)
+    parts, table, weight, swap, gain = lax.optimization_barrier(
+        (parts, table, weight, swap, gain)
+    )
     parts = over(parts, ("sec", "dev"), columns)
     outbound, base = dispatch(parts, table, me)
     inbound = over(outbound, "dev", halves)
     weighted = expert_layer(
-        inbound, norm_gain, weight, swap, gate_proj[0], up_proj[0], down_proj[0]
+        inbound, gain, weight, swap, gate_proj[0], up_proj[0], down_proj[0]
     )
     returned = over(weighted, "dev", halves)
     moe_parts = over(combine(returned, table, column, cols, rows), ("sec", "dev"), columns)

time: 126 us -> 115 us (0.913)
  blocking collectives: 59.9 us -> 75 us
  waiting for transfers between devices: 18.2 us -> 9.85 us
  Pallas kernels: 17 us -> 9.65 us
  starting transfers between devices: 21.8 us -> 15.4 us
  matrix products: 2.2 us -> 0 us
  local copies, waits for them, and re-layouts: 4.32 us -> 2.35 us
    all_to_all x3 -> x4, blocking collectives: 59.9 us -> 75 us  [over(): lax.all_to_all(x, axis, 0, 0, tiled=True, axis_index_groups=groups_of)]
    all_to_all x2 -> x1, waiting for transfers between devices: 18.2 us -> 9.85 us  [over(): lax.all_to_all(x, axis, 0, 0, tiled=True, axis_index_groups=groups_of)]
    all_to_all x2 -> x1, starting transfers between devices: 17.4 us -> 11.7 us  [over(): lax.all_to_all(x, axis, 0, 0, tiled=True, axis_index_groups=groups_of)]
    pallas_call x4 -> x5, Pallas kernels: 14.8 us -> 9.19 us  [the longest x1 4.57 us: expert_layer(): pl.pallas_call(expert_kernel, out_shape=pltpu.VMEM(inbound.shape, jnp.bfl...]
    pallas_call x1, Pallas kernels: 2.24 us -> 0.46 us  [project(): pl.pallas_call(functools.partial(project_kernel, groups=groups), out_shap...]
    unnamed x15 -> x12, local copies, waits for them, and re-layouts: 1.61 us -> 0.02 us
  transfers between devices with their start and end apart: 3 -> 2, of which waited for: 2 -> 1; matrix products, arithmetic and copies ran while one was open for 1% -> 2% of each run, Pallas kernels for 2% -> 1%
where the time goes in v4:
time: 115 us; the launch traced here: 114 us
  blocking collectives  75 us (65%)
  starting transfers between devices  15.4 us (13%)
  waiting for transfers between devices  9.85 us (9%)
  Pallas kernels  9.65 us (8%)
  local copies, waits for them, and re-layouts  2.35 us (2%)
  other arithmetic  1.31 us (1%)
    all_to_all x4, blocking collectives, over(): lax.all_to_all(x, axis, 0, 0, tiled=True, axis_index_groups=groups_of)  75 us
    all_to_all x1, starting transfers between devices, over(): lax.all_to_all(x, axis, 0, 0, tiled=True, axis_index_groups=groups_of)  11.7 us
    all_to_all x1, waiting for transfers between devices, over(): lax.all_to_all(x, axis, 0, 0, tiled=True, axis_index_groups=groups_of)  9.85 us
    pallas_call x1, Pallas kernels, expert_layer(): pl.pallas_call(expert_kernel, out_shape=pltpu.VMEM(inbound.shape, jnp.bfl...  4.57 us
    ppermute x1, starting transfers between devices, shards(): lax.ppermute(jnp.concatenate([out_proj, wanted], axis=1), 'dev', facing)  3.74 us
    pallas_call x1, Pallas kernels, attend(): pl.pallas_call(attend_kernel, out_shape=pltpu.VMEM(queries.shape, jnp.bfl...  2.58 us
  transfers between devices with their start and end apart: 2, of which 1 were waited for; matrix products, arithmetic and copies ran while one was open for 2% of the time, Pallas kernels for 1%

profile of v4, /device:TPU:1, one launch (start us, length us, event | category | flops | bytes accessed | tf_op | source)
XLA Modules:
  0.0 113.8 jit_solution(2917974934774282039)
XLA Ops:
  0.0 0.0 copy-start.2
  0.0 0.0 copy-start.1
  0.0 0.0 copy-start
  0.0 0.0 copy-start.5
  0.0 0.0 copy-start.4
  0.0 0.0 copy-start.3
  0.0 2.6 %attend.1 = bf16[2,2048]{1,0:T(2,128)(2,1)S(1)} custom-call(s32[2]{0:T(128)} %lengths_ref.1, bf16[2,2048]{1,0:T(2,128)(2,1)} %queries_hbm.1, bf16[2,1,512,128]{3,2,1,0:T(8,128)(2,1)} %keys_hbm.1, bf16[2,1,512,128]{3,2,1,0:T(8,128)(2,1)} %values_hbm.1), custom_call_target="tpu_custom_call" | custom-call | tf_op jit(solution)/shard_map/attend/pallas_call | solution.py:91
  2.6 1.1 broadcast_in_dim.2
  3.7 11.7 %all-to-all-start = ((bf16[64,2,2048]{2,1,0:T(2,128)(2,1)}), bf16[64,2,2048]{2,1,0:T(2,128)(2,1)}, u32[]{:S(2)}, u32[]{:S(2)}) async-start(bf16[64,2,2048]{2,1,0:T(2,128)(2,1)} %broadcast_in_dim.2), calls=%async_computation | async-start | bytes 1048576 | tf_op jit(solution)/shard_map/all_to_all | solution.py:380
  15.4 0.0 copy-done.1
  15.4 0.0 copy-done
  15.4 0.7 pad_maximum_fusion
  16.1 3.7 %collective-permute-start = (bf16[32,2176]{1,0:T(8,128)(2,1)}, bf16[32,2176]{1,0:T(8,128)(2,1)S(1)}, u32[]{:S(2)}, u32[]{:S(2)}) collective-permute-start(bf16[32,2176]{1,0:T(8,128)(2,1)} %pad_maximum_fusion), channel_id=1, source_target_pairs={{0,64},{1,65},{2,66},{3,67},{4,68},{5,69},{6,70},{7,71},{8,72},{9,... | collective-permute-start | bytes 417800 | tf_op jit(solution)/shard_map/ppermute | solution.py:386
  19.9 0.0 copy-done.5
  19.9 0.0 copy-done.2
  19.9 0.0 copy-done.4
  19.9 0.0 copy-done.3
  19.9 0.8 routing.1
  20.7 9.8 %all-to-all-done = bf16[64,2,2048]{2,1,0:T(2,128)(2,1)} async-done(((bf16[64,2,2048]{2,1,0:T(2,128)(2,1)}), bf16[64,2,2048]{2,1,0:T(2,128)(2,1)}, u32[]{:S(2)}, u32[]{:S(2)}) %all-to-all-start) | async-done | bytes 524320 | tf_op jit(solution)/shard_map/all_to_all | solution.py:380
  30.5 1.2 %reshape.16.heads_ref = bf16[128,2048]{1,0:T(8,128)(2,1)S(1)} reshape(bf16[64,2,2048]{2,1,0:T(2,128)(2,1)} %all-to-all-done) | data formatting | bytes 1048576 | tf_op jit(solution)/shard_map/reshape | solution.py:392
  31.8 0.0 collective-permute-done.other_ref
  31.8 0.5 project.1
  32.3 25.2 %all_to_all.25.parts_ref = bf16[8,64,128]{2,1,0:T(8,128)(2,1)S(1)} all-to-all(bf16[8,64,128]{2,1,0:T(8,128)(2,1)S(1)} %project.1), channel_id=1, replica_groups={{0,64,128,192,256,320,384,448},{1,65,129,193,257,321,385,449},{2,66,130..., dimensions={0} | all-to-all | bytes 262144 | tf_op jit(solution)/shard_map/all_to_all | solution.py:380
  57.5 0.7 dispatch.1
  58.2 18.3 %all_to_all.26.inbound_ref = bf16[64,24,128]{2,1,0:T(8,128)(2,1)S(1)} all-to-all(bf16[64,24,128]{2,1,0:T(8,128)(2,1)S(1)} %get-tuple-element.25), channel_id=1, replica_groups={{0,1,2,3,4,5,6,7,8,9,10,11,12,13,14,15,16,17,18,19,20,21,22,23,24,25,26..., dimensions={0} | all-to-all | bytes 786432 | tf_op jit(solution)/shard_map/all_to_all | solution.py:380
  76.5 4.6 %expert_layer.1 = bf16[64,24,128]{2,1,0:T(8,128)(2,1)S(1)} custom-call(bf16[64,24,128]{2,1,0:T(8,128)(2,1)S(1)} %all_to_all.26.inbound_ref, bf16[1,4096]{1,0:T(2,128)(2,1)S(1)} %reshape.18.gain_ref, f32[64,1]{1,0:T(8,128)S(1)} %get-tuple-element.27.weight_ref, bf16[512,512]{1,0:T(8,128)(2,1)S(1)} %get-tuple-element.28.swap_ref, bf16[192,4096]{1,0:T(8,128)(2,1)} %bitcast.16, ...), custom_call_target="tpu_custom_call" | custom-call | tf_op jit(solution)/shard_map/expert_layer/pallas_call | solution.py:308
  81.1 15.3 %all_to_all.27.returned_ref = bf16[64,24,128]{2,1,0:T(8,128)(2,1)S(1)} all-to-all(bf16[64,24,128]{2,1,0:T(8,128)(2,1)S(1)} %expert_layer.1), channel_id=1, replica_groups={{0,1,2,3,4,5,6,7,8,9,10,11,12,13,14,15,16,17,18,19,20,21,22,23,24,25,26..., dimensions={0} | all-to-all | bytes 786432 | tf_op jit(solution)/shard_map/all_to_all | solution.py:380
  96.4 0.6 combine.1
  97.0 16.2 %all_to_all.28 = bf16[8,32,256]{2,1,0:T(8,128)(2,1)S(1)} all-to-all(bf16[8,32,256]{2,1,0:T(8,128)(2,1)S(1)} %combine.1), channel_id=1, replica_groups={{0,64,128,192,256,320,384,448},{1,65,129,193,257,321,385,449},{2,66,130..., dimensions={0} | all-to-all | bytes 262144 | tf_op jit(solution)/shard_map/all_to_all | solution.py:380
  113.2 0.6 fusion
  (3 shorter events, 0.0 us)
Async XLA Ops:
  0.0 19.9 %copy-start.2 = (s32[256,8]{0,1:T(8,128)S(1)}, s32[256,8]{0,1:T(8,128)}, u32[]{:S(2)}) copy-start(s32[256,8]{0,1:T(8,128)} %param.20) | copy-start | bytes 24580
  0.0 15.4 %copy-start.1 = (bf16[256,32]{0,1:T(8,128)(2,1)S(1)}, bf16[256,32]{0,1:T(8,128)(2,1)}, u32[]{:S(2)}) copy-start(bf16[256,32]{0,1:T(8,128)(2,1)} %param.18) | copy-start | bytes 49156
  0.0 15.4 %copy-start = (bf16[32,2048]{1,0:T(8,128)(2,1)S(1)}, bf16[32,2048]{1,0:T(8,128)(2,1)}, u32[]{:S(2)}) copy-start(bf16[32,2048]{1,0:T(8,128)(2,1)} %own_ref.1) | copy-start | bytes 393220
  0.0 19.9 %copy-start.5 = (bf16[4096]{0:T(1024)(128)(2,1)S(1)}, bf16[4096]{0:T(1024)(128)(2,1)}, u32[]{:S(2)}) copy-start(bf16[4096]{0:T(1024)(128)(2,1)} %param.19) | copy-start | bytes 24580
  0.0 19.9 %copy-start.4 = (s32[128]{0:T(128)S(1)}, s32[128]{0:T(128)}, u32[]{:S(2)}) copy-start(s32[128]{0:T(128)} %param.22) | copy-start | bytes 1540
  0.0 19.9 %copy-start.3 = (f32[256,8]{0,1:T(8,128)S(1)}, f32[256,8]{0,1:T(8,128)}, u32[]{:S(2)}) copy-start(f32[256,8]{0,1:T(8,128)} %param.21) | copy-start | bytes 24580
  3.7 26.8 %all-to-all-start = ((bf16[64,2,2048]{2,1,0:T(2,128)(2,1)}), bf16[64,2,2048]{2,1,0:T(2,128)(2,1)}, u32[]{:S(2)}, u32[]{:S(2)}) async-start(bf16[64,2,2048]{2,1,0:T(2,128)(2,1)} %broadcast_in_dim.2), calls=%async_computation | async-start | bytes 1048576 | tf_op jit(solution)/shard_map/all_to_all | solution.py:380
  16.1 15.7 %collective-permute-start = (bf16[32,2176]{1,0:T(8,128)(2,1)}, bf16[32,2176]{1,0:T(8,128)(2,1)S(1)}, u32[]{:S(2)}, u32[]{:S(2)}) collective-permute-start(bf16[32,2176]{1,0:T(8,128)(2,1)} %pad_maximum_fusion), channel_id=1, source_target_pairs={{0,64},{1,65},{2,66},{3,67},{4,68},{5,69},{6,70},{7,71},{8,72},{9,... | collective-permute-start | bytes 417800 | tf_op jit(solution)/shard_map/ppermute | solution.py:386
